TPU v7x, 256 devices: a whole 4x4x8 slice. The times are simulated.
256 devices in a mesh: gx: 8 (over y, z_hi), gy: 8 (over z_lo, core), gz: 4 (over x).
Axes of the slice: x: 4, y: 4, z: 8 (z_hi: 2, z_lo: 4; z = z_hi * 4 + z_lo), core: 2. Of those that a mesh axis runs over, the one named last changes fastest.
Arguments:
- latents: bfloat16 [262144, 128], P(('gx', 'gy', 'gz')), may hold values from -6 to 6
- grad_mixed: bfloat16 [262144, 128], P(('gx', 'gy', 'gz')), may hold values from -6 to 6
- neighbours: int32 [262144, 16], P(('gx', 'gy', 'gz')), may hold values from 0 to 1535, as said below
- send_list: int32 [1024, 64], P(('gx', 'gy', 'gz')), may hold values from 0 to 1023
- cluster: int32 [262144], P(('gx', 'gy', 'gz')), may hold values from 0 to 255
- w_send: bfloat16 [128, 128], replicated, may hold values from -0.5 to 0.5
- w_recv: bfloat16 [128, 128], replicated, may hold values from -0.5 to 0.5
- w_edge: bfloat16 [128, 128], replicated, may hold values from -0.5 to 0.5
- edge_gain: float32 [128], replicated, may hold values from 0.1 to 1.9
- w_self: bfloat16 [128, 128], replicated, may hold values from -0.5 to 0.5
- w_agg: bfloat16 [128, 128], replicated, may hold values from -0.5 to 0.5
- w_node: bfloat16 [128, 128], replicated, may hold values from -0.5 to 0.5
- node_gain: float32 [128], replicated, may hold values from 0.1 to 1.9
- w_pool_in: bfloat16 [128, 128], replicated, may hold values from -0.25 to 0.25
- w_pool_out: bfloat16 [128, 128], replicated, may hold values from -0.5 to 0.5
Outputs:
- mixed: bfloat16 [262144, 128], P(('gx', 'gy', 'gz'))
- grad_latents: float32 [262144, 128], P(('gx', 'gy', 'gz'))
- grad_matrices: float32 [8, 128, 128], replicated
- grad_gains: float32 [2, 128], replicated
Inputs may be any that keep to these rules, and one draw needn't show every extreme that they name: Entries below 1024 are a device's own particles; entry 1024 + k * 64 + r is row r of its k-th received cell in the order of the steps. The table is cut into tiles of 64 rows; a device's particle r, of own tile t = r // 64, has all its neighbours in own tile t, own tile (t + 1) mod (16), or received tile t mod (8), the rows from 1024 + that tile's number * 64 on. `send_list`: indices of the sending device's own particles. `cluster`: cluster numbers count within the particle's group of gz devices.
All inputs are finite; a program needn't handle non-finite values.
Results may differ from a plain program's by a relative error of at most 0.025.
Values may be sent and summed in bfloat16 or wider, within the bound.
A program may use at most 128 MiB of HBM per device.

v0:
```python
import jax
import jax.numpy as jnp
from jax import lax
from jax.sharding import PartitionSpec as P

EPS = 1e-05


def with_halo(block, sides, width):
    for axis, dim in sides:
        count = lax.axis_size(axis)
        forward = [(i, i + 1) for i in range(count - 1)]
        forward.append((count - 1, 0))
        backward = [(target, source) for source, target in forward]
        low = lax.ppermute(
            lax.slice_in_dim(block, block.shape[dim] - width, None, axis=dim), axis, forward
        )
        high = lax.ppermute(lax.slice_in_dim(block, 0, width, axis=dim), axis, backward)
        block = jnp.concatenate([low, block, high], axis=dim)
    return block


def matmul_f32(left, right):
    return jnp.dot(left, right, preferred_element_type=jnp.float32)


def silu_slope(values):
    logistic = jax.nn.sigmoid(values)
    return logistic * (1.0 + values * (1.0 - logistic))


def norm_rows(values):
    centred = values - jnp.mean(values, axis=-1, keepdims=True)
    inv_std = lax.rsqrt(jnp.mean(centred * centred, axis=-1, keepdims=True) + EPS)
    return (centred * inv_std, inv_std)


def norm_back(grad_normed, normed, inv_std):
    first_mean = jnp.mean(grad_normed, axis=-1, keepdims=True)
    second_mean = jnp.mean(grad_normed * normed, axis=-1, keepdims=True)
    return (grad_normed - first_mean - normed * second_mean) * inv_std


def matrix_rescale(mats):
    return mats * lax.rsqrt(jnp.mean(mats * mats, axis=(1, 2), keepdims=True) + 1e-06)


def block_split(row_count):
    block_rows = min(512, row_count)
    return (block_rows, row_count // block_rows)


def tile_size(row_count):
    return min(128, row_count // 16)


def build_windows(proj_ext, row_count):
    tile_rows = tile_size(row_count)
    feat_width = proj_ext.shape[1]
    own_tiles = proj_ext[:row_count].reshape(-1, tile_rows, feat_width)
    ghost_tiles = proj_ext[row_count:].reshape(-1, tile_rows, feat_width)
    return jnp.concatenate(
        [
            own_tiles,
            jnp.roll(own_tiles, -1, 0),
            jnp.concatenate([ghost_tiles, ghost_tiles], axis=0),
        ],
        axis=1,
    )


def fold_windows(window_grads, row_count):
    tile_rows = tile_size(row_count)
    feat_width = window_grads.shape[-1]
    half_tiles = window_grads.shape[0] // 2
    own_part = window_grads[:, :tile_rows] + jnp.roll(
        window_grads[:, tile_rows : 2 * tile_rows], 1, 0
    )
    ghost_part = (
        window_grads[:half_tiles, 2 * tile_rows :] + window_grads[half_tiles:, 2 * tile_rows :]
    )
    return jnp.concatenate(
        [own_part.reshape(-1, feat_width), ghost_part.reshape(-1, feat_width)], axis=0
    )


def window_onehot(index_block, block_index, row_count):
    tile_rows = tile_size(row_count)
    tiles_per = index_block.shape[0] // tile_rows
    first_tile = block_index * tiles_per
    tile_ids = first_tile + jnp.arange(tiles_per, dtype=jnp.int32)
    grouped = index_block.reshape(tiles_per, -1)
    which_part = jnp.where(
        grouped >= row_count, 2, jnp.where(grouped // tile_rows == tile_ids[:, None], 0, 1)
    )
    local_slot = grouped % tile_rows + tile_rows * which_part
    slot_ids = jnp.arange(3 * tile_rows, dtype=jnp.int32)
    onehot = (local_slot[:, :, None] == slot_ids[None, None, :]).astype(jnp.bfloat16)
    return (onehot, tiles_per, first_tile)


def edge_block(windows, recv_block, index_block, block_index, row_count, w_edge):
    feat_width = windows.shape[-1]
    onehot, tiles_per, first_tile = window_onehot(index_block, block_index, row_count)
    window_block = lax.dynamic_slice_in_dim(windows, first_tile, tiles_per, 0)
    picked = jnp.einsum("tek,tkd->ted", onehot, window_block, preferred_element_type=jnp.float32)
    picked = picked.reshape(recv_block.shape[0], -1, feat_width)
    pre_edge = (picked + recv_block[:, None, :].astype(jnp.float32)).reshape(-1, feat_width)
    act_edge = jax.nn.silu(pre_edge).astype(jnp.bfloat16)
    message = matmul_f32(act_edge, w_edge)
    normed, inv_std = norm_rows(message)
    return (pre_edge, act_edge, normed, inv_std)


def fine_forward(
    latents, proj_ext, neighbours, w_recv, w_edge, edge_gain, w_self, w_agg, w_node, node_gain
):
    row_count, feat_width = latents.shape
    block_rows, blocks = block_split(row_count)
    recv_rows = matmul_f32(latents, w_recv).astype(jnp.bfloat16)
    windows = build_windows(proj_ext, row_count)

    def one_block(inputs):
        block_index, index_block, recv_block = inputs
        pre_edge, act_edge, normed, inv_std = edge_block(
            windows, recv_block, index_block, block_index, row_count, w_edge
        )
        summed = (normed * edge_gain).reshape(block_rows, -1, feat_width).sum(axis=1)
        return (summed, (pre_edge, act_edge, normed, inv_std))

    block_ids = jnp.arange(blocks, dtype=jnp.int32)
    gathered, edge_state = lax.map(
        one_block,
        (
            block_ids,
            neighbours.reshape(blocks, block_rows, -1),
            recv_rows.reshape(blocks, block_rows, feat_width),
        ),
    )
    agg_rows = gathered.reshape(row_count, feat_width).astype(jnp.bfloat16)
    pre_node = matmul_f32(latents, w_self) + matmul_f32(agg_rows, w_agg)
    act_node = jax.nn.silu(pre_node).astype(jnp.bfloat16)
    normed_node, inv_node = norm_rows(matmul_f32(act_node, w_node))
    fine_latents = (latents.astype(jnp.float32) + normed_node * node_gain).astype(jnp.bfloat16)
    return (
        fine_latents,
        (recv_rows, agg_rows, pre_node, act_node, normed_node, inv_node, edge_state),
    )


def fine_backward(
    grad_fine,
    latents,
    neighbours,
    saved_state,
    w_send,
    w_recv,
    w_edge,
    edge_gain,
    w_self,
    w_agg,
    w_node,
    node_gain,
):
    recv_rows, agg_rows, pre_node, act_node, normed_node, inv_node, edge_state = saved_state
    row_count, feat_width = latents.shape
    neigh_count = neighbours.shape[1]
    block_rows, blocks = block_split(row_count)
    grad_node_gain = jnp.sum(grad_fine * normed_node, axis=0)
    grad_out = norm_back(grad_fine * node_gain, normed_node, inv_node).astype(jnp.bfloat16)
    grad_w_node = matmul_f32(act_node.T, grad_out)
    grad_pre_node = (matmul_f32(grad_out, w_node.T) * silu_slope(pre_node)).astype(jnp.bfloat16)
    grad_w_self = matmul_f32(latents.T, grad_pre_node)
    grad_w_agg = matmul_f32(agg_rows.T, grad_pre_node)
    grad_lat = grad_fine + matmul_f32(grad_pre_node, w_self.T)
    grad_agg = matmul_f32(grad_pre_node, w_agg.T)

    def one_block(carried, inputs):
        grad_w_edge, grad_edge_gain = carried
        block_index, index_block, agg_block, pre_edge, act_edge, normed, inv_std = inputs
        grad_message = jnp.broadcast_to(
            agg_block[:, None, :], (block_rows, neigh_count, feat_width)
        ).reshape(-1, feat_width)
        grad_edge_gain = grad_edge_gain + jnp.sum(grad_message * normed, axis=0)
        grad_edge = norm_back(grad_message * edge_gain, normed, inv_std).astype(jnp.bfloat16)
        grad_w_edge = grad_w_edge + matmul_f32(act_edge.T, grad_edge)
        grad_pre_b = (matmul_f32(grad_edge, w_edge.T) * silu_slope(pre_edge)).astype(jnp.bfloat16)
        onehot, tiles_per, first_tile = window_onehot(index_block, block_index, row_count)
        window_grad = jnp.einsum(
            "tek,ted->tkd",
            onehot,
            grad_pre_b.reshape(tiles_per, -1, feat_width),
            preferred_element_type=jnp.float32,
        )
        grad_pre = lax.optimization_barrier(grad_pre_b).astype(jnp.float32)
        grad_recv = grad_pre.reshape(block_rows, neigh_count, feat_width).sum(axis=1)
        return ((grad_w_edge, grad_edge_gain), (grad_recv, window_grad))

    initial = (
        jnp.zeros((feat_width, feat_width), jnp.float32),
        jnp.zeros((feat_width,), jnp.float32),
    )
    pre_all, act_all, normed_all, inv_all = edge_state
    block_ids = jnp.arange(blocks, dtype=jnp.int32)
    scanned = (
        block_ids,
        neighbours.reshape(blocks, block_rows, -1),
        grad_agg.reshape(blocks, block_rows, feat_width),
        pre_all,
        act_all,
        normed_all,
        inv_all,
    )
    (grad_w_edge, grad_edge_gain), (grad_recv, window_grads) = lax.scan(one_block, initial, scanned)
    tile_rows = tile_size(row_count)
    grad_proj = fold_windows(window_grads.reshape(-1, 3 * tile_rows, feat_width), row_count)
    grad_recv = grad_recv.reshape(row_count, feat_width).astype(jnp.bfloat16)
    grad_w_recv = matmul_f32(latents.T, grad_recv)
    grad_lat = grad_lat + matmul_f32(grad_recv, w_recv.T)
    grad_proj = grad_proj.astype(jnp.bfloat16)
    grad_w_send = matmul_f32(latents.T, grad_proj[:row_count])
    grad_lat = grad_lat + matmul_f32(grad_proj[:row_count], w_send.T)
    matrices = (grad_w_send, grad_w_recv, grad_w_edge, grad_w_self, grad_w_agg, grad_w_node)
    return (grad_lat, grad_proj[row_count:], matrices, (grad_edge_gain, grad_node_gain))


def cluster_forward(pooled, w_pool_in, w_pool_out):
    pooled_b = pooled.astype(jnp.bfloat16)
    pre_pool = matmul_f32(pooled_b, w_pool_in)
    act_pool = jax.nn.silu(pre_pool).astype(jnp.bfloat16)
    delta_rows = matmul_f32(act_pool, w_pool_out).astype(jnp.bfloat16)
    return (pooled_b, pre_pool, act_pool, delta_rows)


def cluster_backward(grad_delta, pre_pool, w_pool_in, w_pool_out):
    grad_delta_b = grad_delta.astype(jnp.bfloat16)
    grad_pre_pool = (matmul_f32(grad_delta_b, w_pool_out.T) * silu_slope(pre_pool)).astype(
        jnp.bfloat16
    )
    grad_pooled = matmul_f32(grad_pre_pool, w_pool_in.T).astype(jnp.bfloat16)
    return (grad_delta_b, grad_pre_pool, grad_pooled)


def rim_rows(padded):
    return jnp.stack(
        [
            padded[0, 1],
            padded[0, 2],
            padded[3, 1],
            padded[3, 2],
            padded[1, 0],
            padded[2, 0],
            padded[1, 3],
            padded[2, 3],
        ]
    )


def slot_cells(pieces):
    ghost_rows, feat_width = (pieces.shape[1], pieces.shape[2])
    first_slot = pieces[0:4].reshape(2, 2, ghost_rows, feat_width)
    second_slot = jnp.swapaxes(pieces[4:8].reshape(2, 2, ghost_rows, feat_width), 0, 1)
    return jnp.stack([first_slot, second_slot], axis=2)


def fold_cells(padded):
    along_x = jnp.stack([padded[0, 1:3, 0], padded[3, 1:3, 0]])
    along_y = jnp.stack([padded[1:3, 0, 1], padded[1:3, 3, 1]], axis=1)
    return (along_x + along_y).reshape(-1, padded.shape[-1])


def per_device(
    latents,
    grad_mixed,
    neighbours,
    send_list,
    cluster,
    w_send,
    w_recv,
    w_edge,
    edge_gain,
    w_self,
    w_agg,
    w_node,
    node_gain,
    w_pool_in,
    w_pool_out,
):
    row_count, feat_width = latents.shape
    ghost_rows = send_list.shape[1]
    share_rows = row_count // 16
    group_rows = share_rows * lax.axis_size("gz")
    flat_send = send_list.reshape(-1)
    sent_lat = latents[flat_send]
    own_proj = matmul_f32(latents, w_send).astype(jnp.bfloat16)
    cell_rows = sent_lat.reshape(2, 2, ghost_rows, feat_width)
    padded = with_halo(cell_rows, (("gx", 0), ("gy", 1)), 1)
    pieces = rim_rows(padded).reshape(8 * ghost_rows, feat_width)
    ghost_proj = matmul_f32(pieces, w_send).astype(jnp.bfloat16)
    proj_ext = jnp.concatenate([own_proj, ghost_proj], axis=0)
    fine_latents, saved_state = fine_forward(
        latents, proj_ext, neighbours, w_recv, w_edge, edge_gain, w_self, w_agg, w_node, node_gain
    )
    labels = jnp.arange(group_rows, dtype=jnp.int32)
    onehot = (cluster[:, None] == labels[None, :]).astype(jnp.bfloat16)

    def pool_rows(values):
        partial_rows = matmul_f32(onehot.T, values)
        return lax.psum_scatter(
            partial_rows.astype(jnp.bfloat16), "gz", scatter_dimension=0, tiled=True
        ).astype(jnp.float32)

    def spread_rows(values):
        return lax.all_gather(values, "gz", axis=0, tiled=True)

    pooled = pool_rows(fine_latents)
    pooled_b, pre_pool, act_pool, delta_rows = cluster_forward(pooled, w_pool_in, w_pool_out)
    mixed_out = (
        fine_latents.astype(jnp.float32) + matmul_f32(onehot, spread_rows(delta_rows))
    ).astype(jnp.bfloat16)
    grad_delta = pool_rows(grad_mixed)
    grad_delta_b, grad_pre_pool, grad_pooled = cluster_backward(
        grad_delta, pre_pool, w_pool_in, w_pool_out
    )
    pooled_own, pre_grad_own, act_own, delta_grad_own = (
        pooled_b,
        grad_pre_pool,
        act_pool,
        grad_delta_b,
    )
    grad_pool_in = matmul_f32(pooled_own.T, pre_grad_own)
    grad_pool_out = matmul_f32(act_own.T, delta_grad_own)
    grad_fine = grad_mixed.astype(jnp.float32) + matmul_f32(onehot, spread_rows(grad_pooled))
    grad_lat, grad_ghost, matrices, gains = fine_backward(
        grad_fine,
        latents,
        neighbours,
        saved_state,
        w_send,
        w_recv,
        w_edge,
        edge_gain,
        w_self,
        w_agg,
        w_node,
        node_gain,
    )
    grad_w_send = matrices[0]
    grad_w_send = grad_w_send + matmul_f32(pieces.T, grad_ghost)
    ghost_back = matmul_f32(grad_ghost, w_send.T)
    slots = slot_cells(ghost_back.reshape(8, ghost_rows, feat_width))
    returned = with_halo(slots.astype(jnp.bfloat16), (("gx", 0), ("gy", 1)), 1).astype(slots.dtype)
    back_rows = fold_cells(returned)
    grad_lat = grad_lat.at[flat_send].add(back_rows)
    grad_scale = float(
        row_count * lax.axis_size("gx") * lax.axis_size("gy") * lax.axis_size("gz")
    ) ** (-0.5)
    local_mats = jnp.stack([grad_w_send] + list(matrices[1:]) + [grad_pool_in, grad_pool_out])
    local_gains = jnp.stack(gains) * grad_scale
    summed_mats, grad_gains = lax.psum((local_mats, local_gains), ("gx", "gy", "gz"))
    grad_matrices = matrix_rescale(summed_mats)
    return (mixed_out, grad_lat, grad_matrices, grad_gains)


def solution(mesh):
    in_specs = (
        P(("gx", "gy", "gz"), None),
        P(("gx", "gy", "gz"), None),
        P(("gx", "gy", "gz"), None),
        P(("gx", "gy", "gz"), None),
        P(("gx", "gy", "gz")),
        P(),
        P(),
        P(),
        P(),
        P(),
        P(),
        P(),
        P(),
        P(),
        P(),
    )
    out_specs = (P(("gx", "gy", "gz"), None), P(("gx", "gy", "gz"), None), P(), P())
    return jax.shard_map(
        per_device, mesh=mesh, in_specs=in_specs, out_specs=out_specs, check_vma=False
    )
```

profile of v0, /device:TPU:1, one launch (start us, length us, event | category | flops | bytes accessed | tf_op | source)
XLA Modules:
  0.0 501.0 jit_solution(13882186338913673572)
XLA Ops:
  9.7 7.8 %collective-permute-start = (bf16[1,2,64,128]{3,2,1,0:T(8,128)(2,1)S(1)}, bf16[1,2,64,128]{3,2,1,0:T(8,128)(2,1)S(1)}, u32[]{:S(2)}, u32[]{:S(2)}) collective-permute-start(bf16[1,2,64,128]{3,2,1,0:T(8,128)(2,1)S(1)} %bitcast.371), channel_id=1, source_target_pairs={{0,32},{32,64},{64,96},{96,128},{128,160},{160,192},{192,224},{224... | collective-permute-start | bytes 98312 | tf_op jit(solution)/shard_map/ppermute | solution.py:15
  17.6 2.5 collective-permute-start.1
  28.9 3.1 collective-permute-done.3
  32.7 46.3 %while.39 = (s32[]{:T(128)}, bf16[2,512,128]{2,1,0:T(8,128)(2,1)S(1)}, f32[2,8192,128]{2,1,0:T(8,128)}, bf16[2,8192,128]{2,1,0:T(8,128)(2,1)}, f32[2,8192,128]{2...) while((s32[]{:T(128)}, ...), condition=%wide.region_4.5_spmd, body=%wide.region_0.4_spmd.sunk | while | flops 696991744 | bytes 214205968 | solution.py:132
  39.1 2.4 multiply_reduce_fusion.9
  41.6 2.5 bitcast_dynamic-update-slice_fusion.8
  44.3 2.9 copy-done.2
  47.9 3.1 copy-done.3
  52.2 2.9 bitcast_reduce_fusion.2
  64.7 2.5 bitcast_dynamic-update-slice_fusion.8
  67.5 2.9 copy-done.2
  71.1 3.1 copy-done.3
  75.4 2.9 bitcast_reduce_fusion.2
  83.4 18.6 %reduce-scatter.3.cloned.1.call-done = bf16[64,128]{1,0:T(8,128)(2,1)} async-done(((bf16[256,128]{1,0:T(8,128)(2,1)}), bf16[64,128]{1,0:T(8,128)(2,1)}) %reduce-scatter.3.cloned.1.call-update) | async-done | bytes 16400 | tf_op jit(solution)/shard_map/reduce_scatter | solution.py:309
  102.9 25.1 %reduce-scatter.5.cloned.1.call-done = bf16[64,128]{1,0:T(8,128)(2,1)} async-done(((bf16[256,128]{1,0:T(8,128)(2,1)}), bf16[64,128]{1,0:T(8,128)(2,1)}) %reduce-scatter.5.cloned.1.call-update) | async-done | bytes 16400 | tf_op jit(solution)/shard_map/reduce_scatter | solution.py:309
  129.6 9.0 %all_gather.7 = bf16[256,128]{1,0:T(8,128)(2,1)S(1)} all-gather(bf16[64,128]{1,0:T(8,128)(2,1)S(1)} %convolution_convert_fusion.6), channel_id=1, replica_groups=mesh['gx'=8,'gy'=8,'gz'=4] {'gz'}, dimensions={0}, use_global_device_ids=true | all-gather | bytes 81920 | tf_op jit(solution)/shard_map/all_gather | solution.py:314
  143.2 78.1 %while.40 = (s32[]{:T(128)}, f32[128,128]{1,0:T(8,128)}, f32[128]{0:T(128)S(1)}, bf16[2,512,128]{2,1,0:T(8,128)(2,1)}, f32[2,8,192,128]{3,2,1,0:T(8,128)}, /*ind...) while((s32[]{:T(128)}, f32[128,128]{1,0:T(8,128)}, ...), condition=%wide.region_16.17_spmd.clone, body=%wide.region_11.16_spmd.clone.sunk | while | flops 972726400 | bytes 72259504 | solution.py:214
  144.6 3.3 fusion.166
  154.5 6.7 %fusion.172 = bf16[8192,128]{1,0:T(8,128)(2,1)S(1)} fusion(f32[1,8192,128]{2,1,0:T(8,128)} %copy-done.1, f32[8192]{0:T(1024)S(1)} %bitcast.343, f32[8192]{0:T(1024)S(1)} %broadcast_multiply_fusion.11, f32[8192]{0:T(1024)S(1)} %div.205, f32[128]{0:T(128)S(1)} %get-tuple-element.742, f32[512,128]{1,0:T(8,128)S(1)} %dynamic-slice_bitcast_fusion.2), kind=kLoop, calls=%fused_computation.58.clone.1 | loop fusion | flops 6291456 | bytes 6652416 | tf_op jit(solution)/shard_map/while/body/eval_jaxpr/convert_element_type | solution.py:185
  161.2 4.1 fusion.173
  171.3 7.9 %fusion.169 = bf16[512,16,128]{2,1,0:T(8,128)(2,1)S(1)} fusion(f32[512,16,128]{2,1,0:T(8,128)} %bitcast.331, f32[512,16]{1,0:T(8,128)S(1)} %mul.545, f32[512,16]{1,0:T(8,128)S(1)} %div.204, f32[512,16]{1,0:T(8,128)S(1)} %broadcast_multiply_fusion.12, f32[128]{0:T(128)S(1)} %get-tuple-element.742, f32[512,128]{1,0:T(8,128)S(1)} %dynamic-slice_bitcast_fusion.2), kind=kLoop, calls=%fused_computation.42.clone.1 | loop fusion | flops 6291456 | bytes 6652416 | tf_op jit(solution)/shard_map/while/body/eval_jaxpr/convert_element_type | solution.py:185
  179.2 2.4 fusion.170
  183.7 3.3 fusion.166
  193.6 6.7 %fusion.172 = bf16[8192,128]{1,0:T(8,128)(2,1)S(1)} fusion(f32[1,8192,128]{2,1,0:T(8,128)} %copy-done.1, f32[8192]{0:T(1024)S(1)} %bitcast.343, f32[8192]{0:T(1024)S(1)} %broadcast_multiply_fusion.11, f32[8192]{0:T(1024)S(1)} %div.205, f32[128]{0:T(128)S(1)} %get-tuple-element.742, f32[512,128]{1,0:T(8,128)S(1)} %dynamic-slice_bitcast_fusion.2), kind=kLoop, calls=%fused_computation.58.clone.1 | loop fusion | flops 6291456 | bytes 6652416 | tf_op jit(solution)/shard_map/while/body/eval_jaxpr/convert_element_type | solution.py:185
  200.3 4.1 fusion.173
  210.3 7.9 %fusion.169 = bf16[512,16,128]{2,1,0:T(8,128)(2,1)S(1)} fusion(f32[512,16,128]{2,1,0:T(8,128)} %bitcast.331, f32[512,16]{1,0:T(8,128)S(1)} %mul.545, f32[512,16]{1,0:T(8,128)S(1)} %div.204, f32[512,16]{1,0:T(8,128)S(1)} %broadcast_multiply_fusion.12, f32[128]{0:T(128)S(1)} %get-tuple-element.742, f32[512,128]{1,0:T(8,128)S(1)} %dynamic-slice_bitcast_fusion.2), kind=kLoop, calls=%fused_computation.42.clone.1 | loop fusion | flops 6291456 | bytes 6652416 | tf_op jit(solution)/shard_map/while/body/eval_jaxpr/convert_element_type | solution.py:185
  218.3 2.4 fusion.170
  232.0 5.8 %collective-permute-start.4 = (bf16[1,2,2,64,128]{4,3,0,2,1:T(8,128)(2,1)S(1)}, bf16[1,2,2,64,128]{4,3,0,2,1:T(8,128)(2,1)S(1)}, u32[]{:S(2)}, u32[]{:S(2)}) collective-permute-start(bf16[1,2,2,64,128]{4,3,0,2,1:T(8,128)(2,1)S(1)} %get-tuple-element.468), channel_id=1, source_target_pairs={{0,32},{32,64},{64,96},{96,128},{128,160},{160,192},{192,224},{224... | collective-permute-start | bytes 196616 | tf_op jit(solution)/shard_map/ppermute | solution.py:15
  242.4 9.6 %all_gather.6 = bf16[256,128]{1,0:T(8,128)(2,1)S(1)} all-gather(bf16[64,128]{1,0:T(8,128)(2,1)S(1)} %convolution_convert_fusion.7), channel_id=1, replica_groups=mesh['gx'=8,'gy'=8,'gz'=4] {'gz'}, dimensions={0}, use_global_device_ids=true | all-gather | bytes 81920 | tf_op jit(solution)/shard_map/all_gather | solution.py:314
  252.1 9.6 %collective-permute-start.6 = (bf16[4,1,2,64,128]{4,3,0,2,1:T(8,128)(2,1)S(1)}, bf16[4,1,2,64,128]{4,3,0,2,1:T(8,128)(2,1)S(1)}, u32[]{:S(2)}, u32[]{:S(2)}) collective-permute-start(bf16[4,1,2,64,128]{4,3,0,2,1:T(8,128)(2,1)S(1)} %get-tuple-element.466), channel_id=1, source_target_pairs={{0,4},{4,8},{8,12},{12,16},{16,20},{20,24},{24,28},{28,0},{1,5},{5... | collective-permute-start | bytes 393224 | tf_op jit(solution)/shard_map/ppermute | solution.py:15
  263.2 75.8 %psum.15 = f32[2,128]{1,0:T(2,128)} all-reduce(f32[2,128]{1,0:T(2,128)S(1)} %maximum_multiply_fusion), channel_id=1, replica_groups=mesh['gx'=8,'gy'=8,'gz'=4] {'gx','gy','gz'}, use_global_device_ids=true, to_apply=%region_21.22 | all-reduce | flops 256 | bytes 2048 | tf_op jit(solution)/shard_map/psum | solution.py:360
  341.3 149.8 %all-reduce.2.cloned.1.call-done = f32[8,128,128]{1,2,0:T(8,128)} async-done(((f32[8,128,128]{1,2,0:T(8,128)}), f32[8,128,128]{1,2,0:T(8,128)}) %all-reduce.2.cloned.1.call-update) | async-done | bytes 524304 | tf_op jit(solution)/shard_map/psum | solution.py:360
  (303 shorter events, 92.2 us)
Async XLA Ops:
  7.2 12.9 %copy-start = (bf16[128,128]{1,0:T(8,128)(2,1)S(1)}, bf16[128,128]{1,0:T(8,128)(2,1)}, u32[]{:S(2)}) copy-start(bf16[128,128]{1,0:T(8,128)(2,1)} %param.24) | copy-start | bytes 98308
  7.2 25.2 %copy-start.17 = (bf16[128,128]{1,0:T(8,128)(2,1)S(1)}, bf16[128,128]{1,0:T(8,128)(2,1)}, u32[]{:S(2)}) copy-start(bf16[128,128]{1,0:T(8,128)(2,1)} %param.26) | copy-start | bytes 98308
  7.2 25.2 %copy-start.23 = (f32[128]{0:T(128)S(1)}, f32[128]{0:T(128)}, u32[]{:S(2)}) copy-start(f32[128]{0:T(128)} %param.27) | copy-start | bytes 1540
  7.2 94.8 %reduce-scatter.3.cloned.1.call-start = ((), (), s32[]{:S(2)}) async-start(), calls=%async_computation.2 | async-start | bytes 81920 | tf_op jit(solution)/shard_map/reduce_scatter | solution.py:309
  8.0 15.6 %copy-start.37 = (s32[256,1]{0,1:T(1,128)}, s32[256,1]{0,1:T(1,128)S(1)}, u32[]{:S(2)}) copy-start(s32[256,1]{0,1:T(1,128)S(1)} %compare_select_fusion) | copy-start | bytes 3076
  9.7 16.1 %collective-permute-start = (bf16[1,2,64,128]{3,2,1,0:T(8,128)(2,1)S(1)}, bf16[1,2,64,128]{3,2,1,0:T(8,128)(2,1)S(1)}, u32[]{:S(2)}, u32[]{:S(2)}) collective-permute-start(bf16[1,2,64,128]{3,2,1,0:T(8,128)(2,1)S(1)} %bitcast.371), channel_id=1, source_target_pairs={{0,32},{32,64},{64,96},{96,128},{128,160},{160,192},{192,224},{224... | collective-permute-start | bytes 98312 | tf_op jit(solution)/shard_map/ppermute | solution.py:15
  17.6 8.3 %collective-permute-start.1 = (bf16[1,2,64,128]{3,2,1,0:T(8,128)(2,1)S(1)}, bf16[1,2,64,128]{3,2,1,0:T(8,128)(2,1)S(1)}, u32[]{:S(2)}, u32[]{:S(2)}) collective-permute-start(bf16[1,2,64,128]{3,2,1,0:T(8,128)(2,1)S(1)} %bitcast.370), channel_id=1, source_target_pairs={{32,0},{64,32},{96,64},{128,96},{160,128},{192,160},{224,192},{0,2... | collective-permute-start | bytes 98312 | tf_op jit(solution)/shard_map/ppermute | solution.py:18
  25.9 3.0 collective-permute-start.2
  27.5 4.5 collective-permute-start.3
  32.4 46.6 %copy-start.30 = (bf16[128,128]{1,0:T(8,128)(2,1)S(1)}, bf16[128,128]{1,0:T(8,128)(2,1)}, u32[]{:S(2)}) copy-start(bf16[128,128]{1,0:T(8,128)(2,1)} %param.29) | copy-start | bytes 98308
  79.0 60.7 %copy-start.14 = (bf16[2,512,128]{2,1,0:T(8,128)(2,1)}, bf16[2,512,128]{2,1,0:T(8,128)(2,1)S(1)}, u32[]{:S(2)}) copy-start(bf16[2,512,128]{2,1,0:T(8,128)(2,1)S(1)} %get-tuple-element.339) | copy-start | bytes 786436
  79.0 23.1 %copy-start.29 = (bf16[128,128]{1,0:T(8,128)(2,1)S(1)}, bf16[128,128]{1,0:T(8,128)(2,1)}, u32[]{:S(2)}) copy-start(bf16[128,128]{1,0:T(8,128)(2,1)} %param.32) | copy-start | bytes 98308
  79.0 49.0 %copy-start.43 = (bf16[128,128]{1,0:T(8,128)(2,1)S(1)}, bf16[128,128]{1,0:T(8,128)(2,1)}, u32[]{:S(2)}) copy-start(bf16[128,128]{1,0:T(8,128)(2,1)} %param.33) | copy-start | bytes 98308
  79.2 60.6 %copy-start.21 = (f32[1024,128]{1,0:T(8,128)}, f32[1024,128]{1,0:T(8,128)S(1)}, u32[]{:S(2)}) copy-start(f32[1024,128]{1,0:T(8,128)S(1)} %convolution_add_fusion.3) | copy-start | bytes 1572868
  79.2 60.6 %copy-start.42 = (bf16[128,128]{1,0:T(8,128)(2,1)S(1)}, bf16[128,128]{1,0:T(8,128)(2,1)}, u32[]{:S(2)}) copy-start(bf16[128,128]{1,0:T(8,128)(2,1)} %param.30) | copy-start | bytes 98308
  80.7 59.5 %copy-start.27 = (bf16[1024,128]{0,1:T(8,128)(2,1)}, bf16[1024,128]{0,1:T(8,128)(2,1)S(1)}, u32[]{:S(2)}) copy-start(bf16[1024,128]{0,1:T(8,128)(2,1)S(1)} %add_convert_fusion) | copy-start | bytes 786436
  81.9 46.1 %reduce-scatter.5.cloned.1.call-start = ((), (), s32[]{:S(2)}) async-start(), calls=%async_computation.3 | async-start | bytes 81920 | tf_op jit(solution)/shard_map/reduce_scatter | solution.py:309
  83.2 407.9 %all-reduce.2.cloned.1.call-start = ((), (), s32[]{:S(2)}) async-start(), calls=%async_computation.4 | async-start | bytes 1048576 | tf_op jit(solution)/shard_map/psum | solution.py:360
  102.9 26.0 %copy-start.35 = (f32[64,128]{1,0:T(8,128)}, f32[64,128]{1,0:T(8,128)S(1)}, u32[]{:S(2)}) copy-start(f32[64,128]{1,0:T(8,128)S(1)} %fusion.70) | copy-start | bytes 98308
  143.2 23.9 %copy-start.6 = (s32[2,512,16]{2,1,0:T(8,128)}, s32[2,512,16]{2,1,0:T(8,128)S(1)}, u32[]{:S(2)}) copy-start(s32[2,512,16]{2,1,0:T(8,128)S(1)} %get-tuple-element.747) | copy-start | bytes 196612 | tf_op jit(solution)/shard_map/while
  182.3 23.9 %copy-start.6 = (s32[2,512,16]{2,1,0:T(8,128)}, s32[2,512,16]{2,1,0:T(8,128)S(1)}, u32[]{:S(2)}) copy-start(s32[2,512,16]{2,1,0:T(8,128)S(1)} %get-tuple-element.747) | copy-start | bytes 196612 | tf_op jit(solution)/shard_map/while
  209.4 8.9 %copy-start.11 = (f32[128,128]{1,0:T(8,128)S(1)}, f32[128,128]{1,0:T(8,128)}, u32[]{:S(2)}) copy-start(f32[128,128]{1,0:T(8,128)} %get-tuple-element.718) | copy-start | bytes 196612 | tf_op jit(solution)/shard_map/while
  225.8 14.3 %copy-start.31 = (bf16[128,128]{1,0:T(8,128)(2,1)S(1)}, bf16[128,128]{1,0:T(8,128)(2,1)}, u32[]{:S(2)}) copy-start(bf16[128,128]{1,0:T(8,128)(2,1)} %param.25) | copy-start | bytes 98308
  229.3 32.4 %copy-start.28 = (bf16[1024,128]{0,1:T(8,128)(2,1)S(1)}, bf16[1024,128]{0,1:T(8,128)(2,1)}, u32[]{:S(2)}) copy-start(bf16[1024,128]{0,1:T(8,128)(2,1)} %copy-done.27) | copy-start | bytes 786436
  229.3 32.4 %copy-start.45 = (s32[1024]{0:T(1024)S(1)}, s32[1024]{0:T(1024)}, u32[]{:S(2)}) copy-start(s32[1024]{0:T(1024)} %param.23) | copy-start | bytes 12292
  230.0 33.3 %copy-start.40 = (f32[128]{0:T(128)S(1)}, f32[128]{0:T(128)}, u32[]{:S(2)}) copy-start(f32[128]{0:T(128)} %get-tuple-element.401) | copy-start | bytes 1540
  232.0 107.1 %copy-start.38 = (s32[256,1]{0,1:T(1,128)S(1)}, s32[256,1]{0,1:T(1,128)}, u32[]{:S(2)}) copy-start(s32[256,1]{0,1:T(1,128)} %copy-done.37) | copy-start | bytes 3076
  232.0 20.0 %collective-permute-start.4 = (bf16[1,2,2,64,128]{4,3,0,2,1:T(8,128)(2,1)S(1)}, bf16[1,2,2,64,128]{4,3,0,2,1:T(8,128)(2,1)S(1)}, u32[]{:S(2)}, u32[]{:S(2)}) collective-permute-start(bf16[1,2,2,64,128]{4,3,0,2,1:T(8,128)(2,1)S(1)} %get-tuple-element.468), channel_id=1, source_target_pairs={{0,32},{32,64},{64,96},{96,128},{128,160},{160,192},{192,224},{224... | collective-permute-start | bytes 196616 | tf_op jit(solution)/shard_map/ppermute | solution.py:15
  237.8 14.2 %collective-permute-start.5 = (bf16[1,2,2,64,128]{4,3,0,2,1:T(8,128)(2,1)S(1)}, bf16[1,2,2,64,128]{4,3,0,2,1:T(8,128)(2,1)S(1)}, u32[]{:S(2)}, u32[]{:S(2)}) collective-permute-start(bf16[1,2,2,64,128]{4,3,0,2,1:T(8,128)(2,1)S(1)} %get-tuple-element.469), channel_id=1, source_target_pairs={{32,0},{64,32},{96,64},{128,96},{160,128},{192,160},{224,192},{0,2... | collective-permute-start | bytes 196616 | tf_op jit(solution)/shard_map/ppermute | solution.py:18
  252.1 87.0 %collective-permute-start.6 = (bf16[4,1,2,64,128]{4,3,0,2,1:T(8,128)(2,1)S(1)}, bf16[4,1,2,64,128]{4,3,0,2,1:T(8,128)(2,1)S(1)}, u32[]{:S(2)}, u32[]{:S(2)}) collective-permute-start(bf16[4,1,2,64,128]{4,3,0,2,1:T(8,128)(2,1)S(1)} %get-tuple-element.466), channel_id=1, source_target_pairs={{0,4},{4,8},{8,12},{12,16},{16,20},{20,24},{24,28},{28,0},{1,5},{5... | collective-permute-start | bytes 393224 | tf_op jit(solution)/shard_map/ppermute | solution.py:15
  261.7 77.3 %collective-permute-start.7 = (bf16[4,1,2,64,128]{4,3,0,2,1:T(8,128)(2,1)S(1)}, bf16[4,1,2,64,128]{4,3,0,2,1:T(8,128)(2,1)S(1)}, u32[]{:S(2)}, u32[]{:S(2)}) collective-permute-start(bf16[4,1,2,64,128]{4,3,0,2,1:T(8,128)(2,1)S(1)} %get-tuple-element.467), channel_id=1, source_target_pairs={{4,0},{8,4},{12,8},{16,12},{20,16},{24,20},{28,24},{0,28},{5,1},{9... | collective-permute-start | bytes 393224 | tf_op jit(solution)/shard_map/ppermute | solution.py:18
  341.3 153.2 %copy-start.8 = (f32[1024,128]{1,0:T(8,128)}, f32[1024,128]{1,0:T(8,128)S(1)}, u32[]{:S(2)}) copy-start(f32[1024,128]{1,0:T(8,128)S(1)} %scatter_fusion) | copy-start | bytes 1572868
  (42 other events, 174.4 us)
Sparse Core Ops, SparseCore 0:
  82.0 19.9 reduce-scatter.2
  105.1 22.8 reduce-scatter.4
  232.1 258.9 all-reduce.1
where the time goes:
time: 504 us; the launch traced here: 501 us
  waiting for transfers between devices  198 us (39%)
  blocking collectives  94.4 us (19%)
  other arithmetic  71.8 us (14%)
  local copies, waits for them, and re-layouts  45.1 us (9%)
  matrix products  43.9 us (9%)
  starting transfers between devices  29.9 us (6%)
  between operations  14.6 us (3%)
    psum x1, waiting for transfers between devices, per_device(): lax.psum((local_mats, local_gains), ('gx', 'gy', 'gz'))  150 us
    psum x1, blocking collectives, per_device(): lax.psum((local_mats, local_gains), ('gx', 'gy', 'gz'))  75.8 us
    reduce_scatter x2, waiting for transfers between devices, pool_rows(): lax.psum_scatter(partial_rows.astype(jnp.bfloat16), 'gz', scatter_dimensi...  43.7 us
    dot_general x34, matrix products, matmul_f32(): return jnp.dot(left, right, preferred_element_type=jnp.float32)  35.3 us
    convert_element_type x4, other arithmetic, one_block(): norm_back(grad_message * edge_gain, normed, inv_std).astype(jnp.bfloat16)  29.2 us
    ppermute x4, starting transfers between devices, with_halo(): lax.ppermute(lax.slice_in_dim(block, block.shape[dim] - width, None, axis...  24.9 us
    all_gather x2, blocking collectives, spread_rows(): return lax.all_gather(values, 'gz', axis=0, tiled=True)  18.6 us
    while x52, local copies, waits for them, and re-layouts  17.2 us
  transfers between devices with their start and end apart: 11, of which 5 were waited for; matrix products, arithmetic and copies ran while one was open for 3% of the time, Pallas kernels for 0%

commit v1 on v0

v1 whole, which is shorter than its diff:
```python
import functools

import jax
import jax.numpy as jnp
from jax import lax
from jax.experimental import pallas as pl
from jax.experimental.pallas import tpu as pltpu
from jax.sharding import PartitionSpec as P

EPS = 1e-05
W = 128
ROWS = 1024
NEIGH = 16
TILE = 64
PAIRS = ROWS // W
GHOSTS = 512
CLUSTERS = 256
SLOTS = 192
CHUNK = 256
STEPS = TILE * NEIGH // CHUNK
GAIN_ROWS = 16
F32 = jnp.float32
BF16 = jnp.bfloat16
MESH = pl.DeviceIdType.MESH


def mm(a, b):
    return lax.dot_general(a, b, (((1,), (0,)), ((), ())), preferred_element_type=F32)


def nt(a, b):
    return lax.dot_general(a, b, (((1,), (1,)), ((), ())), preferred_element_type=F32)


def sigmoid(v):
    return 0.5 * jnp.tanh(0.5 * v) + 0.5


def mean0(v):
    return jnp.sum(v, axis=0, keepdims=True) * (1.0 / W)


def norm_cols(z):
    centred = z - mean0(z)
    inv = lax.rsqrt(mean0(centred * centred) + EPS)
    return centred * inv, inv


def low_half():
    return lax.broadcasted_iota(jnp.int32, (W, W), 1) < TILE


def swap(v):
    return pltpu.roll(v, TILE, 1)


def spread_halves(block, low):
    other = swap(block)
    return jnp.where(low, block, other), jnp.where(low, other, block)


def column_of(row):
    return jnp.transpose(jnp.broadcast_to(row, (W, W)))


def kernel(sizes, *refs):
    (lat, gm, nb, send, clus, w_send, w_recv, w_edge, w_self, w_agg, w_node, w_pin, w_pout, egain, ngain) = refs[:15]
    mixed_o, grad_o, mats_o, gains_o = refs[15:19]
    (sbuf, ghost, ret, backbuf, pg, pf, early, early_in, early_mid, early_out, late, late_in, late_mid, late_out,
     lat_t, gm_t, oh_send, oh_clus, tab, tab_sh, gtab, gtab_sh, recv_t, wsa_t,
     oh_all, act_all, slope_all, norm_all, inv_all, sum_t, agg_t, an_t, nslope_t, nn_t, ninv_t, fine_t, gfine_t,
     gy_t, gpn_t, gc_t, grecv_t, gz_tmp, gp_tmp, gp_own, gp_ghost, dw_edge, sums) = refs[19:66]
    (halo_s, halo_r, ret_s, ret_r, pg_s, pg_r, pf_s, pf_r,
     e1s, e1r, e2s, e2r, e3s, e3r, l1s, l1r, l2s, l2r, l3s, l3r) = refs[66:]
    n_x, n_y, n_z = sizes
    n_a, n_b = n_x * n_z, n_y
    c_rows = 4 * W // n_a
    gx, gy, gz = lax.axis_index("gx"), lax.axis_index("gy"), lax.axis_index("gz")
    x_up = (lax.rem(gx + 1, n_x), gy, gz)
    x_low = (lax.rem(gx + n_x - 1, n_x), gy, gz)
    y_up = (gx, lax.rem(gy + 1, n_y), gz)
    y_low = (gx, lax.rem(gy + n_y - 1, n_y), gz)
    rank_a = ((gx // 2) * 2 + lax.rem(gy, 2)) * n_z + gz
    rank_b = lax.rem(gx, 2) * (n_y // 2) + gy // 2

    def z_peer(k):
        return lax.rem(gz + k, n_z)

    def a_peer(k):
        return lax.rem(rank_a + k, n_a)

    def a_dev(r):
        yc = r // n_z
        return ((yc // 2) * 2 + lax.rem(gx, 2), (gy // 2) * 2 + lax.rem(yc, 2), lax.rem(r, n_z))

    def b_peer(k):
        return lax.rem(rank_b + k, n_b)

    def b_dev(r):
        return ((gx // 2) * 2 + r // (n_y // 2), lax.rem(r, n_y // 2) * 2 + lax.rem(gy, 2), gz)

    def remote(src, dst, s, r, dev):
        return pltpu.make_async_remote_copy(
            src_ref=src, dst_ref=dst, send_sem=s, recv_sem=r, device_id=dev, device_id_type=MESH
        )

    def drain(ref, sem):
        pltpu.make_async_copy(ref, ref, sem).wait()

    barrier = pltpu.get_barrier_semaphore()
    for dev in (x_up, x_low, y_up, y_low):
        pl.semaphore_signal(barrier, inc=1, device_id=dev, device_id_type=MESH)

    def greet_a(k, c):
        pl.semaphore_signal(barrier, inc=1, device_id=a_dev(a_peer(k)), device_id_type=MESH)
        return c

    def greet_b(k, c):
        pl.semaphore_signal(barrier, inc=1, device_id=b_dev(b_peer(k)), device_id_type=MESH)
        return c

    lax.fori_loop(1, n_a, greet_a, 0)
    lax.fori_loop(1, n_b, greet_b, 0)

    lane_row = lax.broadcasted_iota(jnp.int32, (TILE, W), 1)
    send_f = send[...].astype(F32)
    for q in range(4):
        col = jnp.transpose(jnp.broadcast_to(send_f[q : q + 1, :], (W, TILE))).astype(jnp.int32)
        for b in range(PAIRS):
            hot = jnp.where(col == lane_row + b * W, 1.0, 0.0).astype(BF16)
            oh_send[q * TILE : (q + 1) * TILE, b * W : (b + 1) * W] = hot
    cells = mm(oh_send[...], lat[...]).astype(BF16)
    for slot, q in enumerate((2, 3, 0, 1, 1, 3, 0, 2)):
        sbuf[slot * TILE : (slot + 1) * TILE, :] = cells[q * TILE : (q + 1) * TILE, :]
    pl.semaphore_wait(barrier, 4 + n_a - 1 + n_b - 1)
    halo_to = (x_up, x_low, y_up, y_low)
    halo = [
        remote(sbuf.at[pl.ds(q * W, W)], ghost.at[pl.ds(q * W, W)], halo_s.at[q], halo_r.at[q], halo_to[q])
        for q in range(4)
    ]
    for c in halo:
        c.start()

    eye = jnp.where(
        lax.broadcasted_iota(jnp.int32, (W, W), 0) == lax.broadcasted_iota(jnp.int32, (W, W), 1), 1.0, 0.0
    ).astype(BF16)
    gm_t[...] = nt(eye, gm[...]).astype(BF16)
    cl_id = lax.broadcasted_iota(jnp.int32, (CLUSTERS, W), 0)
    for b in range(PAIRS):
        oh_clus[:, b * W : (b + 1) * W] = jnp.where(clus[:, b * W : (b + 1) * W] == cl_id, 1.0, 0.0).astype(BF16)

    def pool_send(buf, sems_s, sems_r):
        def go(k, c):
            to = (gx, gy, z_peer(k))
            remote(buf.at[gz], buf.at[gz], sems_s.at[k], sems_r.at[gz], to).start()
            return c

        lax.fori_loop(1, n_z, go, 0)

    def pool_wait(buf, sems_s, sems_r):
        def go(k, c):
            src = lax.rem(gz + n_z - k, n_z)
            remote(buf.at[gz], buf.at[src], sems_s.at[k], sems_r.at[src], (gx, gy, z_peer(k))).wait_recv()
            return c

        lax.fori_loop(1, n_z, go, 0)

    def pool_done(buf, sems_s, sems_r):
        def go(k, c):
            remote(buf.at[gz], buf.at[gz], sems_s.at[k], sems_r.at[gz], (gx, gy, z_peer(k))).wait_send()
            return c

        lax.fori_loop(1, n_z, go, 0)

    pg[gz] = nt(gm_t[...], oh_clus[...]).astype(BF16)
    pool_send(pg, pg_s, pg_r)

    lat_t[...] = nt(eye, lat[...]).astype(BF16)
    we_t = jnp.transpose(w_edge[...].astype(F32)).astype(BF16)
    wsend_t = jnp.transpose(w_send[...].astype(F32)).astype(BF16)
    wrecv_t = jnp.transpose(w_recv[...].astype(F32)).astype(BF16)
    wnode_t = jnp.transpose(w_node[...].astype(F32)).astype(BF16)
    wsa_t[:, :W] = jnp.transpose(w_self[...].astype(F32)).astype(BF16)
    wsa_t[:, W:] = jnp.transpose(w_agg[...].astype(F32)).astype(BF16)
    tab[...] = mm(wsend_t, lat_t[...]).astype(BF16)
    lat_roll = jnp.concatenate([lat[TILE:, :], lat[:TILE, :]], axis=0)
    tab_sh[...] = nt(wsend_t, lat_roll).astype(BF16)
    recv_t[...] = mm(wrecv_t, lat_t[...]).astype(BF16).astype(F32)
    eg = column_of(egain[...])
    ng = column_of(ngain[...])

    for c in halo:
        c.wait()
    gh = ghost[...]
    gtab[...] = nt(wsend_t, gh).astype(BF16)
    gtab_sh[...] = nt(wsend_t, jnp.concatenate([gh[TILE:, :], gh[:TILE, :]], axis=0)).astype(BF16)

    def forward(u, carry):
        low = low_half()
        slot_id = lax.broadcasted_iota(jnp.int32, (SLOTS, W), 0)
        at = pl.multiple_of(u * W, W)
        at_g = pl.multiple_of(lax.rem(u, GHOSTS // W) * W, W)
        picks = nb[:, pl.ds(at, W)]
        low8 = low[:8, :]
        first, second = picks[:8, :], picks[8:, :]
        picks_of = (jnp.where(low8, first, swap(second)), jnp.where(low8, swap(first), second))
        recv_of = spread_halves(recv_t[:, pl.ds(at, W)], low)
        sums_of = []
        for half in range(2):
            t = 2 * u + half
            chosen = picks_of[half]
            local = jnp.where(chosen >= ROWS, (chosen & (TILE - 1)) + 2 * TILE, (chosen - t * TILE) & (ROWS - 1))
            own, far = (tab, gtab) if half == 0 else (tab_sh, gtab_sh)
            window = jnp.concatenate([own[:, pl.ds(at, W)], far[:, pl.ds(at_g, TILE)]], axis=1)
            total = None
            for q in range(STEPS):
                lanes = slice(q * CHUNK, (q + 1) * CHUNK)
                hot = jnp.concatenate(
                    [jnp.where(local[c : c + 1, :] == slot_id, 1.0, 0.0).astype(BF16) for c in (2 * q, 2 * q + 1)], axis=1
                )
                oh_all[t, :, lanes] = hot
                pre = mm(window, hot) + jnp.concatenate([recv_of[half]] * 2, axis=1)
                s = sigmoid(pre)
                act = pre * s
                act_b = act.astype(BF16)
                act_all[t, :, lanes] = act_b
                slope_all[t, :, lanes] = (s + act * (1.0 - s)).astype(BF16)
                normed, inv = norm_cols(mm(we_t, act_b))
                norm_all[t, :, lanes] = normed.astype(BF16)
                inv_all[t, :, lanes] = inv
                part = normed[:, :W] + normed[:, W:]
                total = part if total is None else total + part
            sums_of.append(total + swap(total))
        total = jnp.where(low, sums_of[0], sums_of[1])
        sum_t[:, pl.ds(at, W)] = total
        agg_b = (total * eg).astype(BF16)
        agg_t[:, pl.ds(at, W)] = agg_b
        lat_b = lat_t[:, pl.ds(at, W)]
        pn = mm(wsa_t[...], jnp.concatenate([lat_b, agg_b], axis=0))
        s = sigmoid(pn)
        an = pn * s
        an_b = an.astype(BF16)
        an_t[:, pl.ds(at, W)] = an_b
        nslope_t[:, pl.ds(at, W)] = s + an * (1.0 - s)
        nn, ninv = norm_cols(mm(wnode_t, an_b))
        nn_t[:, pl.ds(at, W)] = nn
        ninv_t[:, pl.ds(at, W)] = ninv
        fine_t[:, pl.ds(at, W)] = (lat_b.astype(F32) + nn * ng).astype(BF16)
        return carry

    lax.fori_loop(0, PAIRS, forward, 0)

    pf[gz] = nt(fine_t[...], oh_clus[...]).astype(BF16)
    pool_send(pf, pf_s, pf_r)
    wpin_t = jnp.transpose(w_pin[...].astype(F32)).astype(BF16)
    wpout_t = jnp.transpose(w_pout[...].astype(F32)).astype(BF16)
    pool_wait(pg, pg_s, pg_r)
    gd = pg[0].astype(F32)
    for k in range(1, n_z):
        gd = gd + pg[k].astype(F32)
    gd_b = gd.astype(BF16)
    gac = mm(w_pout[...], gd_b)
    pool_wait(pf, pf_s, pf_r)
    pooled = pf[0].astype(F32)
    for k in range(1, n_z):
        pooled = pooled + pf[k].astype(F32)
    pooled_b = pooled.astype(BF16)
    pc = mm(wpin_t, pooled_b)
    s = sigmoid(pc)
    ac = pc * s
    ac_b = ac.astype(BF16)
    delta_b = mm(wpout_t, ac_b).astype(BF16)
    gpc_b = (gac * (s + ac * (1.0 - s))).astype(BF16)
    gpool_b = mm(w_pin[...], gpc_b).astype(BF16)
    both = jnp.concatenate([delta_b, gpool_b], axis=0)
    dw_pin = nt(pooled_b, gpc_b) * (1.0 / n_z)
    dw_pout = nt(ac_b, gd_b) * (1.0 / n_z)

    sums[...] = jnp.zeros_like(sums)

    def node_back(u, carry):
        at = pl.multiple_of(u * W, W)
        added = mm(both, oh_clus[:, pl.ds(at, W)])
        mixed = fine_t[:, pl.ds(at, W)].astype(F32) + added[:W, :]
        mixed_o[pl.ds(at, W), :] = jnp.transpose(mixed).astype(BF16)
        gf = gm_t[:, pl.ds(at, W)].astype(F32) + added[W:, :]
        gfine_t[:, pl.ds(at, W)] = gf
        nn = nn_t[:, pl.ds(at, W)]
        sums[1] += gf * nn
        gn = gf * ng
        gy_b = ((gn - mean0(gn) - nn * mean0(gn * nn)) * ninv_t[:, pl.ds(at, W)]).astype(BF16)
        gy_t[:, pl.ds(at, W)] = gy_b
        gpn_b = (mm(w_node[...], gy_b) * nslope_t[:, pl.ds(at, W)]).astype(BF16)
        gpn_t[:, pl.ds(at, W)] = gpn_b
        ga = mm(w_agg[...], gpn_b)
        sums[0] += ga * sum_t[:, pl.ds(at, W)]
        g = ga * eg
        gc_t[:, pl.ds(at, W)] = g - mean0(g)
        return carry

    lax.fori_loop(0, PAIRS, node_back, 0)

    def put(buf, index, mat, width):
        per = W // c_rows
        buf[index * per : (index + 1) * per, :c_rows, :] = mat.reshape(per, c_rows, W).astype(BF16)

    def reduce_out(buf, into, s, r):
        into[rank_a] = buf[rank_a]

        def go(k, c):
            to = a_peer(k)
            remote(buf.at[to], into.at[rank_a], s, r, a_dev(to)).start()
            return c

        lax.fori_loop(1, n_a, go, 0)

    def reduce_mid(buf, into, mid, s, r, s2, r2):
        drain(into.at[pl.ds(0, n_a - 1)], r)
        total = into[0].astype(F32)
        for k in range(1, n_a):
            total = total + into[k].astype(F32)
        mid[rank_b] = total.astype(BF16)

        def go(k, c):
            remote(mid.at[rank_b], mid.at[rank_b], s2, r2, b_dev(b_peer(k))).start()
            return c

        lax.fori_loop(1, n_b, go, 0)

    def gather_out(mid, out, s2, r2, s3, r3):
        drain(mid.at[pl.ds(0, n_b - 1)], r2)
        total = mid[0].astype(F32)
        for k in range(1, n_b):
            total = total + mid[k].astype(F32)
        out[rank_a] = total.astype(BF16)

        def go(k, c):
            remote(out.at[rank_a], out.at[rank_a], s3, r3, a_dev(a_peer(k))).start()
            return c

        lax.fori_loop(1, n_a, go, 0)

    def finish(buf, mid, out, s, s2, s3, r3):
        drain(out.at[pl.ds(0, n_a - 1)], r3)
        drain(buf.at[pl.ds(0, n_a - 1)], s)
        drain(mid.at[pl.ds(0, n_b - 1)], s2)
        drain(out.at[pl.ds(0, n_a - 1)], s3)

    def row_sums(v):
        hi = v.astype(BF16)
        lo = (v - hi.astype(F32)).astype(BF16)
        ones = jnp.ones((GAIN_ROWS, W), BF16)
        return nt(ones, hi) + nt(ones, lo)

    dw_sa = nt(jnp.concatenate([lat_t[...], agg_t[...]], axis=0), gpn_t[...])
    put(early, 0, dw_sa[:W, :], c_rows)
    put(early, 1, dw_sa[W:, :], c_rows)
    put(early, 2, nt(an_t[...], gy_t[...]), c_rows)
    put(early, 3, dw_pin, c_rows)
    which = lax.broadcasted_iota(jnp.int32, (GAIN_ROWS, W), 0)
    gain_rows = jnp.where(which == 0, row_sums(sums[0]), row_sums(sums[1])).astype(BF16)
    for k in range(n_a):
        early[k, c_rows:, :] = gain_rows
    reduce_out(early, early_in, e1s, e1r)

    gp_own[...] = jnp.zeros_like(gp_own)
    gp_ghost[...] = jnp.zeros_like(gp_ghost)
    dw_edge[...] = jnp.zeros_like(dw_edge)

    def backward(u, carry):
        low = low_half()
        at = pl.multiple_of(u * W, W)
        at_g = pl.multiple_of(lax.rem(u, GHOSTS // W) * W, W)
        gc_of = spread_halves(gc_t[:, pl.ds(at, W)], low)
        back_of = []
        for half in range(2):
            t = 2 * u + half
            gc = jnp.concatenate([gc_of[half]] * 2, axis=1)
            total = None
            for q in range(STEPS):
                lanes = slice(q * CHUNK, (q + 1) * CHUNK)
                normed = norm_all[t, :, lanes].astype(F32)
                gz_b = ((gc - normed * mean0(gc * normed)) * inv_all[t, :, lanes]).astype(BF16)
                gz_tmp[half, :, lanes] = gz_b
                gpre = mm(w_edge[...], gz_b) * slope_all[t, :, lanes].astype(F32)
                gp_tmp[half, :, lanes] = gpre.astype(BF16)
                part = gpre[:, :W] + gpre[:, W:]
                total = part if total is None else total + part
            dw_edge[...] += nt(act_all[t], gz_tmp[half])
            window = nt(oh_all[t], gp_tmp[half])
            gp_own[pl.ds(at + half * TILE, W), :] += window[:W, :]
            gp_ghost[pl.ds(at_g + half * TILE, TILE), :] += window[W:, :]
            back_of.append(total + swap(total))
        grecv_t[:, pl.ds(at, W)] = jnp.where(low, back_of[0], back_of[1]).astype(BF16)
        return carry

    lax.fori_loop(0, PAIRS // 2, backward, 0)
    reduce_mid(early, early_in, early_mid, e1s, e1r, e2s, e2r)
    lax.fori_loop(PAIRS // 2, PAIRS, backward, 0)
    gather_out(early_mid, early_out, e2s, e2r, e3s, e3r)

    backbuf[...] = gp_ghost[...].astype(BF16)
    back_to = (x_low, x_up, y_low, y_up)
    back = [
        remote(backbuf.at[pl.ds(q * W, W)], ret.at[pl.ds(q * W, W)], ret_s.at[q], ret_r.at[q], back_to[q])
        for q in range(4)
    ]
    for c in back:
        c.start()

    gp_own[:TILE, :] += gp_own[ROWS:, :]
    own_b = gp_own[:ROWS, :].astype(BF16)
    ghost_t = nt(eye, ghost[...]).astype(BF16)
    put(late, 0, mm(lat_t[...], own_b) + mm(ghost_t, backbuf[...]), c_rows)
    put(late, 1, nt(lat_t[...], grecv_t[...]), c_rows)
    put(late, 2, dw_edge[...], c_rows)
    put(late, 3, dw_pout, c_rows)
    reduce_out(late, late_in, l1s, l1r)

    gfine_t[...] += (
        mm(w_self[...], gpn_t[...]) + mm(w_recv[...], grecv_t[...]) + nt(w_send[...], own_b)
    )
    for c in back:
        c.wait()
    side_a = jnp.concatenate([ret[q * TILE : (q + 1) * TILE, :] for q in (2, 3, 0, 1)], axis=0)
    side_b = jnp.concatenate([ret[q * TILE : (q + 1) * TILE, :] for q in (6, 4, 7, 5)], axis=0)
    ret_t = (nt(w_send[...], side_a) + nt(w_send[...], side_b)).astype(BF16)
    reduce_mid(late, late_in, late_mid, l1s, l1r, l2s, l2r)
    gfine_t[...] += mm(ret_t, oh_send[...])
    for b in range(PAIRS):
        grad_o[b * W : (b + 1) * W, :] = jnp.transpose(gfine_t[:, b * W : (b + 1) * W])
    gather_out(late_mid, late_out, l2s, l2r, l3s, l3r)

    def emit(out, index, place):
        per = W // c_rows
        mat = out[index * per : (index + 1) * per, :c_rows, :].astype(F32).reshape(W, W)
        mats_o[place] = mat * lax.rsqrt(jnp.mean(mat * mat, keepdims=True) + 1e-06)

    finish(early, early_mid, early_out, e1s, e2s, e3s, e3r)
    for index, place in enumerate((3, 4, 5, 6)):
        emit(early_out, index, place)
    scale = float(ROWS * n_x * n_y * n_z) ** (-0.5)
    gains_o[...] = early_out[0, c_rows : c_rows + 2, :].astype(F32) * scale
    pool_done(pg, pg_s, pg_r)
    pool_done(pf, pf_s, pf_r)
    finish(late, late_mid, late_out, l1s, l2s, l3s, l3r)
    for index, place in enumerate((0, 1, 2, 7)):
        emit(late_out, index, place)


def solution(mesh):
    sizes = tuple(mesh.shape[name] for name in ("gx", "gy", "gz"))
    n_a, n_b, n_z = sizes[0] * sizes[2], sizes[1], sizes[2]
    c_rows = 4 * W // n_a
    tiles = ROWS // TILE
    edges = TILE * NEIGH
    v = pltpu.VMEM
    dma = pltpu.SemaphoreType.DMA

    def reduce_bufs(rows):
        return [v((n_a, rows, W), BF16), v((n_a, rows, W), BF16), v((n_b, rows, W), BF16), v((n_a, rows, W), BF16)]

    scratch = [
        v((GHOSTS, W), BF16),
        v((GHOSTS, W), BF16),
        v((GHOSTS, W), BF16),
        v((GHOSTS, W), BF16),
        v((n_z, W, CLUSTERS), BF16),
        v((n_z, W, CLUSTERS), BF16),
        *reduce_bufs(c_rows + GAIN_ROWS),
        *reduce_bufs(c_rows),
        v((W, ROWS), BF16),
        v((W, ROWS), BF16),
        v((4 * TILE, ROWS), BF16),
        v((CLUSTERS, ROWS), BF16),
        v((W, ROWS), BF16),
        v((W, ROWS), BF16),
        v((W, GHOSTS), BF16),
        v((W, GHOSTS), BF16),
        v((W, ROWS), F32),
        v((W, 2 * W), BF16),
        v((tiles, SLOTS, edges), BF16),
        v((tiles, W, edges), BF16),
        v((tiles, W, edges), BF16),
        v((tiles, W, edges), BF16),
        v((tiles, 1, edges), F32),
        v((W, ROWS), F32),
        v((W, ROWS), BF16),
        v((W, ROWS), BF16),
        v((W, ROWS), F32),
        v((W, ROWS), F32),
        v((1, ROWS), F32),
        v((W, ROWS), BF16),
        v((W, ROWS), F32),
        v((W, ROWS), BF16),
        v((W, ROWS), BF16),
        v((W, ROWS), F32),
        v((W, ROWS), BF16),
        v((2, W, edges), BF16),
        v((2, W, edges), BF16),
        v((ROWS + TILE, W), F32),
        v((GHOSTS, W), F32),
        v((W, W), F32),
        v((2, W, W), F32),
        dma((4,)), dma((4,)), dma((4,)), dma((4,)),
        dma((n_z,)), dma((n_z,)), dma((n_z,)), dma((n_z,)),
        *[dma for _ in range(12)],
    ]

    def step(latents, grad_mixed, neighbours, send_list, cluster, w_send, w_recv, w_edge, edge_gain, w_self, w_agg,
             w_node, node_gain, w_pool_in, w_pool_out):
        return pl.pallas_call(
            functools.partial(kernel, sizes),
            out_shape=(
                jax.ShapeDtypeStruct((ROWS, W), BF16),
                jax.ShapeDtypeStruct((ROWS, W), F32),
                jax.ShapeDtypeStruct((8, W, W), F32),
                jax.ShapeDtypeStruct((2, W), F32),
            ),
            in_specs=[pl.BlockSpec(memory_space=pltpu.VMEM)] * 15,
            out_specs=tuple([pl.BlockSpec(memory_space=pltpu.VMEM)] * 4),
            scratch_shapes=scratch,
            compiler_params=pltpu.CompilerParams(
                collective_id=0, has_side_effects=True, vmem_limit_bytes=60 * 1024 * 1024
            ),
        )(latents, grad_mixed, neighbours.T, send_list, cluster.reshape(1, ROWS), w_send, w_recv, w_edge, w_self,
          w_agg, w_node, w_pool_in, w_pool_out, edge_gain.reshape(1, W), node_gain.reshape(1, W))

    rows = P(("gx", "gy", "gz"), None)
    in_specs = (rows, rows, rows, rows, P(("gx", "gy", "gz"))) + (P(),) * 10
    out_specs = (rows, rows, P(), P())
    return jax.shard_map(step, mesh=mesh, in_specs=in_specs, out_specs=out_specs, check_vma=False)
```

time: 504 us -> 77.2 us (0.15)
  waiting for transfers between devices: 198 us -> 0 us
  blocking collectives: 94.4 us -> 0 us
  Pallas kernels: 0 us -> 72.1 us
  other arithmetic: 71.8 us -> 0 us
  matrix products: 43.9 us -> 0 us
  local copies, waits for them, and re-layouts: 45.1 us -> 4.32 us
  starting transfers between devices: 29.9 us -> 0 us
  between operations: 14.6 us -> 0.66 us
    psum x1 -> x0, waiting for transfers between devices: 150 us -> none  [per_device(): lax.psum((local_mats, local_gains), ('gx', 'gy', 'gz'))]
    psum x1 -> x0, blocking collectives: 75.8 us -> none  [per_device(): lax.psum((local_mats, local_gains), ('gx', 'gy', 'gz'))]
    pallas_call x0 -> x1, Pallas kernels: none -> 72.1 us  [step(): pl.pallas_call(functools.partial(kernel, sizes), out_shape=(jax.ShapeDtyp...]
    dot_general x38 -> x0, matrix products: 43.9 us -> none  [the longest x34 35.3 us: matmul_f32(): return jnp.dot(left, right, preferred_element_type=jnp.float32)]
    reduce_scatter x2 -> x0, waiting for transfers between devices: 43.7 us -> none  [pool_rows(): lax.psum_scatter(partial_rows.astype(jnp.bfloat16), 'gz', scatter_dimensi...]
    convert_element_type x10 -> x0, other arithmetic: 31.8 us -> none  [the longest x4 29.2 us: one_block(): norm_back(grad_message * edge_gain, normed, inv_std).astype(jnp.bfloat16)]
    ppermute x8 -> x0, starting transfers between devices: 29.7 us -> none  [the longest x4 24.9 us: with_halo(): lax.ppermute(lax.slice_in_dim(block, block.shape[dim] - width, None, axis...]
    reduce_sum x14 -> x0, other arithmetic: 25.3 us -> none  [the longest x2 6.62 us: one_block(): grad_edge_gain = grad_edge_gain + jnp.sum(grad_message * normed, axis=0)]
  transfers between devices with their start and end apart: 11 -> 0, of which waited for: 5 -> 0; matrix products, arithmetic and copies ran while one was open for 3% -> 0% of each run, Pallas kernels for 0% -> 0%
where the time goes in v1:
time: 77.2 us; the launch traced here: 77.1 us
  Pallas kernels  72.1 us (93%)
  local copies, waits for them, and re-layouts  4.32 us (6%)
    pallas_call x1, Pallas kernels, step(): pl.pallas_call(functools.partial(kernel, sizes), out_shape=(jax.ShapeDtyp...  72.1 us
    unnamed x10, local copies, waits for them, and re-layouts  4.32 us

profile of v1, /device:TPU:1, one launch (start us, length us, event | category | flops | bytes accessed | tf_op | source)
XLA Modules:
  0.0 77.1 jit_solution(8609272291971755092)
XLA Ops:
  0.6 72.1 %shard_map.174 = (bf16[1024,128]{1,0:T(8,128)(2,1)}, f32[1024,128]{1,0:T(8,128)}, f32[8,128,128]{2,1,0:T(8,128)}, f32[2,128]{1,0:T(2,128)}) custom-call(bf16[1024,128]{1,0:T(8,128)(2,1)} %refs_0_.1, bf16[1024,128]{1,0:T(8,128)(2,1)} %refs_1_.1, s32[16,1024]{1,0:T(8,128)} %bitcast.4, s32[4,64]{1,0:T(4,128)} %refs_3_.1, s32[1,1024]{1,0:T(1,128)} %bitcast.5, ...), custom_call_target="tpu_custom_call" | custom-call | tf_op jit(solution)/shard_map/pallas_call | solution.py:512
  72.7 0.0 copy-start.1
  72.7 1.7 %copy.23 = bf16[1024,128]{1,0:T(8,128)(2,1)} copy(bf16[1024,128]{1,0:T(8,128)(2,1)} %get-tuple-element.8) | data formatting | bytes 524288
  74.5 0.0 copy-done.1
  74.5 0.0 copy-start
  74.5 0.8 %copy.24 = f32[1024,128]{1,0:T(8,128)} copy(f32[1024,128]{1,0:T(8,128)S(1)} %copy-done.1) | data formatting | bytes 1048576
  75.3 0.4 copy-done
  75.7 0.0 copy-start.2
  75.7 0.8 %copy.25 = f32[8,128,128]{2,1,0:T(8,128)} copy(f32[8,128,128]{2,1,0:T(8,128)S(1)} %copy-done) | data formatting | bytes 1048576
  76.5 0.0 copy-done.2
  76.5 0.6 copy.26
Async XLA Ops:
  72.7 1.7 %copy-start.1 = (f32[1024,128]{1,0:T(8,128)S(1)}, f32[1024,128]{1,0:T(8,128)}, u32[]{:S(2)}) copy-start(f32[1024,128]{1,0:T(8,128)} %get-tuple-element.9) | copy-start | bytes 1572868
  74.5 1.2 %copy-start = (f32[8,128,128]{2,1,0:T(8,128)S(1)}, f32[8,128,128]{2,1,0:T(8,128)}, u32[]{:S(2)}) copy-start(f32[8,128,128]{2,1,0:T(8,128)} %get-tuple-element.10) | copy-start | bytes 1572868
  75.7 0.8 %copy-start.2 = (f32[2,128]{1,0:T(2,128)S(1)}, f32[2,128]{1,0:T(2,128)}, u32[]{:S(2)}) copy-start(f32[2,128]{1,0:T(2,128)} %get-tuple-element.11) | copy-start | bytes 3076

commit v2 on v1

--- a/solution.py
+++ b/solution.py
@@ -18,6 +18,7 @@
 SLOTS = 192
 CHUNK = 256
 STEPS = TILE * NEIGH // CHUNK
+NODE = 256
 GAIN_ROWS = 16
 F32 = jnp.float32
 BF16 = jnp.bfloat16
@@ -40,10 +41,33 @@
     return jnp.sum(v, axis=0, keepdims=True) * (1.0 / W)
 
 
-def norm_cols(z):
-    centred = z - mean0(z)
+def norm_centred(centred):
     inv = lax.rsqrt(mean0(centred * centred) + EPS)
     return centred * inv, inv
+
+
+def half_silu(h):
+    t = jnp.tanh(h)
+    up = 1.0 + t
+    act = h * up
+    return act, up + act * (1.0 - t)
+
+
+def centred_pair(w):
+    w_t = jnp.transpose(w.astype(F32))
+    centred = w_t - mean0(w_t)
+    high = centred.astype(BF16)
+    return jnp.concatenate([high, (centred - high.astype(F32)).astype(BF16)], axis=1)
+
+
+def twice(v):
+    return jnp.concatenate([v, v], axis=0)
+
+
+def one_hot(row, ids):
+    wide = jnp.broadcast_to(row, (16, W)).astype(BF16)
+    same = jnp.concatenate([wide] * (ids.shape[0] // 16), axis=0) == ids
+    return jnp.where(same, jnp.ones((), BF16), jnp.zeros((), BF16))
 
 
 def low_half():
@@ -64,14 +88,15 @@
 
 
 def kernel(sizes, *refs):
-    (lat, gm, nb, send, clus, w_send, w_recv, w_edge, w_self, w_agg, w_node, w_pin, w_pout, egain, ngain) = refs[:15]
+    far, near, in_sems = refs[:15], refs[-16:-1], refs[-1]
+    (lat, gm, nb, send, clus, w_send, w_recv, w_edge, w_self, w_agg, w_node, w_pin, w_pout, egain, ngain) = near
     mixed_o, grad_o, mats_o, gains_o = refs[15:19]
     (sbuf, ghost, ret, backbuf, pg, pf, early, early_in, early_mid, early_out, late, late_in, late_mid, late_out,
-     lat_t, gm_t, oh_send, oh_clus, tab, tab_sh, gtab, gtab_sh, recv_t, wsa_t,
+     lat_t, gm_t, oh_send, oh_clus, tab, tab_sh, gtab, gtab_sh, recv_t, wsa_t, we_c, wn_c,
      oh_all, act_all, slope_all, norm_all, inv_all, sum_t, agg_t, an_t, nslope_t, nn_t, ninv_t, fine_t, gfine_t,
-     gy_t, gpn_t, gc_t, grecv_t, gz_tmp, gp_tmp, gp_own, gp_ghost, dw_edge, sums) = refs[19:66]
+     gy_t, gpn_t, gc_t, grecv_t, gz_tmp, gp_tmp, gp_own, gp_ghost, dw_edge, sums) = refs[19:68]
     (halo_s, halo_r, ret_s, ret_r, pg_s, pg_r, pf_s, pf_r,
-     e1s, e1r, e2s, e2r, e3s, e3r, l1s, l1r, l2s, l2r, l3s, l3r) = refs[66:]
+     e1s, e1r, e2s, e2r, e3s, e3r, l1s, l1r, l2s, l2r, l3s, l3r) = refs[68:-16]
     n_x, n_y, n_z = sizes
     n_a, n_b = n_x * n_z, n_y
     c_rows = 4 * W // n_a
@@ -107,6 +132,10 @@
     def drain(ref, sem):
         pltpu.make_async_copy(ref, ref, sem).wait()
 
+    loads = [pltpu.make_async_copy(a, b, in_sems.at[i]) for i, (a, b) in enumerate(zip(far, near))]
+    for i in (3, 0, 1, 4, *range(5, 15), 2):
+        loads[i].start()
+
     barrier = pltpu.get_barrier_semaphore()
     for dev in (x_up, x_low, y_up, y_low):
         pl.semaphore_signal(barrier, inc=1, device_id=dev, device_id_type=MESH)
@@ -123,12 +152,14 @@
     lax.fori_loop(1, n_b, greet_b, 0)
 
     lane_row = lax.broadcasted_iota(jnp.int32, (TILE, W), 1)
+    loads[3].wait()
     send_f = send[...].astype(F32)
     for q in range(4):
         col = jnp.transpose(jnp.broadcast_to(send_f[q : q + 1, :], (W, TILE))).astype(jnp.int32)
         for b in range(PAIRS):
             hot = jnp.where(col == lane_row + b * W, 1.0, 0.0).astype(BF16)
             oh_send[q * TILE : (q + 1) * TILE, b * W : (b + 1) * W] = hot
+    loads[0].wait()
     cells = mm(oh_send[...], lat[...]).astype(BF16)
     for slot, q in enumerate((2, 3, 0, 1, 1, 3, 0, 2)):
         sbuf[slot * TILE : (slot + 1) * TILE, :] = cells[q * TILE : (q + 1) * TILE, :]
@@ -144,10 +175,13 @@
     eye = jnp.where(
         lax.broadcasted_iota(jnp.int32, (W, W), 0) == lax.broadcasted_iota(jnp.int32, (W, W), 1), 1.0, 0.0
     ).astype(BF16)
+    loads[1].wait()
+    loads[4].wait()
     gm_t[...] = nt(eye, gm[...]).astype(BF16)
-    cl_id = lax.broadcasted_iota(jnp.int32, (CLUSTERS, W), 0)
+    cl_id = lax.broadcasted_iota(jnp.int32, (CLUSTERS, W), 0).astype(F32).astype(BF16)
+    clus_f = clus[...].astype(F32)
     for b in range(PAIRS):
-        oh_clus[:, b * W : (b + 1) * W] = jnp.where(clus[:, b * W : (b + 1) * W] == cl_id, 1.0, 0.0).astype(BF16)
+        oh_clus[:, b * W : (b + 1) * W] = one_hot(clus_f[:, b * W : (b + 1) * W], cl_id)
 
     def pool_send(buf, sems_s, sems_r):
         def go(k, c):
@@ -176,12 +210,16 @@
     pool_send(pg, pg_s, pg_r)
 
     lat_t[...] = nt(eye, lat[...]).astype(BF16)
-    we_t = jnp.transpose(w_edge[...].astype(F32)).astype(BF16)
-    wsend_t = jnp.transpose(w_send[...].astype(F32)).astype(BF16)
-    wrecv_t = jnp.transpose(w_recv[...].astype(F32)).astype(BF16)
-    wnode_t = jnp.transpose(w_node[...].astype(F32)).astype(BF16)
-    wsa_t[:, :W] = jnp.transpose(w_self[...].astype(F32)).astype(BF16)
-    wsa_t[:, W:] = jnp.transpose(w_agg[...].astype(F32)).astype(BF16)
+    for i in (*range(5, 15), 2):
+        loads[i].wait()
+    wsend_t = (jnp.transpose(w_send[...].astype(F32)) * 0.5).astype(BF16)
+    wrecv_t = (jnp.transpose(w_recv[...].astype(F32)) * 0.5).astype(BF16)
+    we_c[...] = centred_pair(w_edge[...])
+    wn_c[...] = centred_pair(w_node[...])
+    wsa_t[:, :W] = (jnp.transpose(w_self[...].astype(F32)) * 0.5).astype(BF16)
+    wsa_t[:, W:] = (jnp.transpose(w_agg[...].astype(F32)) * 0.5).astype(BF16)
+    w_edge_h = (w_edge[...].astype(F32) * 0.5).astype(BF16)
+    w_node_h = (w_node[...].astype(F32) * 0.5).astype(BF16)
     tab[...] = mm(wsend_t, lat_t[...]).astype(BF16)
     lat_roll = jnp.concatenate([lat[TILE:, :], lat[:TILE, :]], axis=0)
     tab_sh[...] = nt(wsend_t, lat_roll).astype(BF16)
@@ -189,15 +227,15 @@
     eg = column_of(egain[...])
     ng = column_of(ngain[...])
 
-    for c in halo:
-        c.wait()
-    gh = ghost[...]
-    gtab[...] = nt(wsend_t, gh).astype(BF16)
-    gtab_sh[...] = nt(wsend_t, jnp.concatenate([gh[TILE:, :], gh[:TILE, :]], axis=0)).astype(BF16)
+    def ghost_tables(first):
+        part = slice(first, first + 2 * W)
+        own = ghost[part, :]
+        gtab[:, part] = nt(wsend_t, own).astype(BF16)
+        gtab_sh[:, part] = nt(wsend_t, jnp.concatenate([own[TILE:, :], own[:TILE, :]], axis=0)).astype(BF16)
 
     def forward(u, carry):
         low = low_half()
-        slot_id = lax.broadcasted_iota(jnp.int32, (SLOTS, W), 0)
+        slot_id = lax.broadcasted_iota(jnp.int32, (SLOTS, W), 0).astype(F32).astype(BF16)
         at = pl.multiple_of(u * W, W)
         at_g = pl.multiple_of(lax.rem(u, GHOSTS // W) * W, W)
         picks = nb[:, pl.ds(at, W)]
@@ -210,22 +248,19 @@
             t = 2 * u + half
             chosen = picks_of[half]
             local = jnp.where(chosen >= ROWS, (chosen & (TILE - 1)) + 2 * TILE, (chosen - t * TILE) & (ROWS - 1))
+            local = local.astype(F32)
             own, far = (tab, gtab) if half == 0 else (tab_sh, gtab_sh)
             window = jnp.concatenate([own[:, pl.ds(at, W)], far[:, pl.ds(at_g, TILE)]], axis=1)
             total = None
             for q in range(STEPS):
                 lanes = slice(q * CHUNK, (q + 1) * CHUNK)
-                hot = jnp.concatenate(
-                    [jnp.where(local[c : c + 1, :] == slot_id, 1.0, 0.0).astype(BF16) for c in (2 * q, 2 * q + 1)], axis=1
-                )
+                hot = jnp.concatenate([one_hot(local[c : c + 1, :], slot_id) for c in (2 * q, 2 * q + 1)], axis=1)
                 oh_all[t, :, lanes] = hot
-                pre = mm(window, hot) + jnp.concatenate([recv_of[half]] * 2, axis=1)
-                s = sigmoid(pre)
-                act = pre * s
+                act, slope = half_silu(mm(window, hot) + jnp.concatenate([recv_of[half]] * 2, axis=1))
                 act_b = act.astype(BF16)
                 act_all[t, :, lanes] = act_b
-                slope_all[t, :, lanes] = (s + act * (1.0 - s)).astype(BF16)
-                normed, inv = norm_cols(mm(we_t, act_b))
+                slope_all[t, :, lanes] = slope.astype(BF16)
+                normed, inv = norm_centred(mm(we_c[...], twice(act_b)))
                 norm_all[t, :, lanes] = normed.astype(BF16)
                 inv_all[t, :, lanes] = inv
                 part = normed[:, :W] + normed[:, W:]
@@ -233,22 +268,35 @@
             sums_of.append(total + swap(total))
         total = jnp.where(low, sums_of[0], sums_of[1])
         sum_t[:, pl.ds(at, W)] = total
-        agg_b = (total * eg).astype(BF16)
-        agg_t[:, pl.ds(at, W)] = agg_b
-        lat_b = lat_t[:, pl.ds(at, W)]
-        pn = mm(wsa_t[...], jnp.concatenate([lat_b, agg_b], axis=0))
-        s = sigmoid(pn)
-        an = pn * s
+        agg_t[:, pl.ds(at, W)] = (total * eg).astype(BF16)
+        return carry
+
+    halo[2].wait()
+    halo[3].wait()
+    ghost_tables(2 * W)
+    lax.fori_loop(0, PAIRS // 2, lambda k, c: forward((k // 2) * 4 + 2 + lax.rem(k, 2), c), 0)
+    halo[0].wait()
+    halo[1].wait()
+    ghost_tables(0)
+    lax.fori_loop(0, PAIRS // 2, lambda k, c: forward((k // 2) * 4 + lax.rem(k, 2), c), 0)
+
+    def node_forward(u, carry):
+        at = pl.multiple_of(u * NODE, NODE)
+        lat_b = lat_t[:, pl.ds(at, NODE)]
+        an, slope = half_silu(mm(wsa_t[...], jnp.concatenate([lat_b, agg_t[:, pl.ds(at, NODE)]], axis=0)))
         an_b = an.astype(BF16)
-        an_t[:, pl.ds(at, W)] = an_b
-        nslope_t[:, pl.ds(at, W)] = s + an * (1.0 - s)
-        nn, ninv = norm_cols(mm(wnode_t, an_b))
-        nn_t[:, pl.ds(at, W)] = nn
-        ninv_t[:, pl.ds(at, W)] = ninv
-        fine_t[:, pl.ds(at, W)] = (lat_b.astype(F32) + nn * ng).astype(BF16)
+        an_t[:, pl.ds(at, NODE)] = an_b
+        nslope_t[:, pl.ds(at, NODE)] = slope
+        nn, ninv = norm_centred(mm(wn_c[...], twice(an_b)))
+        nn_t[:, pl.ds(at, NODE)] = nn
+        ninv_t[:, pl.ds(at, NODE)] = ninv
+        fine_t[:, pl.ds(at, NODE)] = (lat_b.astype(F32) + nn * widen(ng)).astype(BF16)
         return carry
 
-    lax.fori_loop(0, PAIRS, forward, 0)
+    def widen(v):
+        return jnp.concatenate([v] * (NODE // W), axis=1)
+
+    lax.fori_loop(0, ROWS // NODE, node_forward, 0)
 
     pf[gz] = nt(fine_t[...], oh_clus[...]).astype(BF16)
     pool_send(pf, pf_s, pf_r)
@@ -279,26 +327,33 @@
     sums[...] = jnp.zeros_like(sums)
 
     def node_back(u, carry):
-        at = pl.multiple_of(u * W, W)
-        added = mm(both, oh_clus[:, pl.ds(at, W)])
-        mixed = fine_t[:, pl.ds(at, W)].astype(F32) + added[:W, :]
-        mixed_o[pl.ds(at, W), :] = jnp.transpose(mixed).astype(BF16)
-        gf = gm_t[:, pl.ds(at, W)].astype(F32) + added[W:, :]
-        gfine_t[:, pl.ds(at, W)] = gf
-        nn = nn_t[:, pl.ds(at, W)]
-        sums[1] += gf * nn
-        gn = gf * ng
-        gy_b = ((gn - mean0(gn) - nn * mean0(gn * nn)) * ninv_t[:, pl.ds(at, W)]).astype(BF16)
-        gy_t[:, pl.ds(at, W)] = gy_b
-        gpn_b = (mm(w_node[...], gy_b) * nslope_t[:, pl.ds(at, W)]).astype(BF16)
-        gpn_t[:, pl.ds(at, W)] = gpn_b
+        at = pl.multiple_of(u * NODE, NODE)
+        added = mm(both, oh_clus[:, pl.ds(at, NODE)])
+        mixed = fine_t[:, pl.ds(at, NODE)].astype(F32) + added[:W, :]
+        for b in range(NODE // W):
+            mixed_o[pl.ds(at + b * W, W), :] = jnp.transpose(mixed[:, b * W : (b + 1) * W]).astype(BF16)
+        gf = gm_t[:, pl.ds(at, NODE)].astype(F32) + added[W:, :]
+        gfine_t[:, pl.ds(at, NODE)] = gf
+        nn = nn_t[:, pl.ds(at, NODE)]
+        sums[1] += narrow(gf * nn)
+        gn = gf * widen(ng)
+        gy_b = ((gn - mean0(gn) - nn * mean0(gn * nn)) * ninv_t[:, pl.ds(at, NODE)]).astype(BF16)
+        gy_t[:, pl.ds(at, NODE)] = gy_b
+        gpn_b = (mm(w_node_h, gy_b) * nslope_t[:, pl.ds(at, NODE)]).astype(BF16)
+        gpn_t[:, pl.ds(at, NODE)] = gpn_b
         ga = mm(w_agg[...], gpn_b)
-        sums[0] += ga * sum_t[:, pl.ds(at, W)]
-        g = ga * eg
-        gc_t[:, pl.ds(at, W)] = g - mean0(g)
+        sums[0] += narrow(ga * sum_t[:, pl.ds(at, NODE)])
+        g = ga * widen(eg)
+        gc_t[:, pl.ds(at, NODE)] = g - mean0(g)
         return carry
 
-    lax.fori_loop(0, PAIRS, node_back, 0)
+    def narrow(v):
+        total = v[:, :W]
+        for b in range(1, NODE // W):
+            total = total + v[:, b * W : (b + 1) * W]
+        return total
+
+    lax.fori_loop(0, ROWS // NODE, node_back, 0)
 
     def put(buf, index, mat, width):
         per = W // c_rows
@@ -382,7 +437,7 @@
                 normed = norm_all[t, :, lanes].astype(F32)
                 gz_b = ((gc - normed * mean0(gc * normed)) * inv_all[t, :, lanes]).astype(BF16)
                 gz_tmp[half, :, lanes] = gz_b
-                gpre = mm(w_edge[...], gz_b) * slope_all[t, :, lanes].astype(F32)
+                gpre = mm(w_edge_h, gz_b) * slope_all[t, :, lanes].astype(F32)
                 gp_tmp[half, :, lanes] = gpre.astype(BF16)
                 part = gpre[:, :W] + gpre[:, W:]
                 total = part if total is None else total + part
@@ -394,19 +449,20 @@
         grecv_t[:, pl.ds(at, W)] = jnp.where(low, back_of[0], back_of[1]).astype(BF16)
         return carry
 
-    lax.fori_loop(0, PAIRS // 2, backward, 0)
-    reduce_mid(early, early_in, early_mid, e1s, e1r, e2s, e2r)
-    lax.fori_loop(PAIRS // 2, PAIRS, backward, 0)
-    gather_out(early_mid, early_out, e2s, e2r, e3s, e3r)
-
-    backbuf[...] = gp_ghost[...].astype(BF16)
     back_to = (x_low, x_up, y_low, y_up)
     back = [
         remote(backbuf.at[pl.ds(q * W, W)], ret.at[pl.ds(q * W, W)], ret_s.at[q], ret_r.at[q], back_to[q])
         for q in range(4)
     ]
-    for c in back:
-        c.start()
+    lax.fori_loop(0, PAIRS // 2, lambda k, c: backward((k // 2) * 4 + lax.rem(k, 2), c), 0)
+    backbuf[: 2 * W, :] = gp_ghost[: 2 * W, :].astype(BF16)
+    back[0].start()
+    back[1].start()
+    reduce_mid(early, early_in, early_mid, e1s, e1r, e2s, e2r)
+    lax.fori_loop(0, PAIRS // 2, lambda k, c: backward((k // 2) * 4 + 2 + lax.rem(k, 2), c), 0)
+    backbuf[2 * W :, :] = gp_ghost[2 * W :, :].astype(BF16)
+    back[2].start()
+    back[3].start()
 
     gp_own[:TILE, :] += gp_own[ROWS:, :]
     own_b = gp_own[:ROWS, :].astype(BF16)
@@ -416,6 +472,7 @@
     put(late, 2, dw_edge[...], c_rows)
     put(late, 3, dw_pout, c_rows)
     reduce_out(late, late_in, l1s, l1r)
+    gather_out(early_mid, early_out, e2s, e2r, e3s, e3r)
 
     gfine_t[...] += (
         mm(w_self[...], gpn_t[...]) + mm(w_recv[...], grecv_t[...]) + nt(w_send[...], own_b)
@@ -425,11 +482,10 @@
     side_a = jnp.concatenate([ret[q * TILE : (q + 1) * TILE, :] for q in (2, 3, 0, 1)], axis=0)
     side_b = jnp.concatenate([ret[q * TILE : (q + 1) * TILE, :] for q in (6, 4, 7, 5)], axis=0)
     ret_t = (nt(w_send[...], side_a) + nt(w_send[...], side_b)).astype(BF16)
+    gfine_t[...] += mm(ret_t, oh_send[...])
     reduce_mid(late, late_in, late_mid, l1s, l1r, l2s, l2r)
-    gfine_t[...] += mm(ret_t, oh_send[...])
     for b in range(PAIRS):
         grad_o[b * W : (b + 1) * W, :] = jnp.transpose(gfine_t[:, b * W : (b + 1) * W])
-    gather_out(late_mid, late_out, l2s, l2r, l3s, l3r)
 
     def emit(out, index, place):
         per = W // c_rows
@@ -443,9 +499,16 @@
     gains_o[...] = early_out[0, c_rows : c_rows + 2, :].astype(F32) * scale
     pool_done(pg, pg_s, pg_r)
     pool_done(pf, pf_s, pf_r)
+    gather_out(late_mid, late_out, l2s, l2r, l3s, l3r)
     finish(late, late_mid, late_out, l1s, l2s, l3s, l3r)
     for index, place in enumerate((0, 1, 2, 7)):
         emit(late_out, index, place)
+
+
+def pass_on(*refs):
+    half = len(refs) // 2
+    for src, dst in zip(refs[:half], refs[half:]):
+        dst[...] = src[...]
 
 
 def solution(mesh):
@@ -479,6 +542,8 @@
         v((W, GHOSTS), BF16),
         v((W, ROWS), F32),
         v((W, 2 * W), BF16),
+        v((W, 2 * W), BF16),
+        v((W, 2 * W), BF16),
         v((tiles, SLOTS, edges), BF16),
         v((tiles, W, edges), BF16),
         v((tiles, W, edges), BF16),
@@ -505,11 +570,14 @@
         dma((4,)), dma((4,)), dma((4,)), dma((4,)),
         dma((n_z,)), dma((n_z,)), dma((n_z,)), dma((n_z,)),
         *[dma for _ in range(12)],
+        v((ROWS, W), BF16), v((ROWS, W), BF16), v((NEIGH, ROWS), jnp.int32), v((4, TILE), jnp.int32),
+        v((1, ROWS), jnp.int32), *[v((W, W), BF16) for _ in range(8)], v((1, W), F32), v((1, W), F32),
+        dma((15,)),
     ]
 
     def step(latents, grad_mixed, neighbours, send_list, cluster, w_send, w_recv, w_edge, edge_gain, w_self, w_agg,
              w_node, node_gain, w_pool_in, w_pool_out):
-        return pl.pallas_call(
+        results = pl.pallas_call(
             functools.partial(kernel, sizes),
             out_shape=(
                 jax.ShapeDtypeStruct((ROWS, W), BF16),
@@ -517,14 +585,22 @@
                 jax.ShapeDtypeStruct((8, W, W), F32),
                 jax.ShapeDtypeStruct((2, W), F32),
             ),
-            in_specs=[pl.BlockSpec(memory_space=pltpu.VMEM)] * 15,
+            in_specs=[pl.BlockSpec(memory_space=pltpu.HBM)] * 15,
             out_specs=tuple([pl.BlockSpec(memory_space=pltpu.VMEM)] * 4),
             scratch_shapes=scratch,
             compiler_params=pltpu.CompilerParams(
-                collective_id=0, has_side_effects=True, vmem_limit_bytes=60 * 1024 * 1024
+                collective_id=0, has_side_effects=True, vmem_limit_bytes=44 * 1024 * 1024
             ),
-        )(latents, grad_mixed, neighbours.T, send_list, cluster.reshape(1, ROWS), w_send, w_recv, w_edge, w_self,
-          w_agg, w_node, w_pool_in, w_pool_out, edge_gain.reshape(1, W), node_gain.reshape(1, W))
+        )(*[pltpu.with_memory_space_constraint(x, pltpu.HBM) for x in (
+            latents, grad_mixed, neighbours.T, send_list, cluster.reshape(1, ROWS), w_send, w_recv, w_edge, w_self,
+            w_agg, w_node, w_pool_in, w_pool_out, edge_gain.reshape(1, W), node_gain.reshape(1, W))])
+        return pl.pallas_call(
+            pass_on,
+            out_shape=tuple(jax.ShapeDtypeStruct(r.shape, r.dtype) for r in results),
+            in_specs=[pl.BlockSpec(memory_space=pltpu.VMEM)] * 4,
+            out_specs=tuple([pl.BlockSpec(memory_space=pltpu.VMEM)] * 4),
+            compiler_params=pltpu.CompilerParams(vmem_limit_bytes=8 * 1024 * 1024),
+        )(*results)
 
     rows = P(("gx", "gy", "gz"), None)
     in_specs = (rows, rows, rows, rows, P(("gx", "gy", "gz"))) + (P(),) * 10

time: 77.2 us -> 63 us (0.82)
  Pallas kernels: 72.1 us -> 62.3 us
  local copies, waits for them, and re-layouts: 4.32 us -> 0 us
    pallas_call x1, Pallas kernels: 72.1 us -> 61.2 us  [step(): pl.pallas_call(functools.partial(kernel, sizes), out_shape=(jax.ShapeDtyp...]
    unnamed x10 -> x0, local copies, waits for them, and re-layouts: 4.32 us -> none
    pallas_call x0 -> x1, Pallas kernels: none -> 1.14 us  [step(): pl.pallas_call(pass_on, out_shape=tuple((jax.ShapeDtypeStruct(r.shape, r....]
where the time goes in v2:
time: 63 us
  Pallas kernels  62.3 us (99%)
  between operations  0.65 us (1%)
    pallas_call x1, Pallas kernels, step(): pl.pallas_call(functools.partial(kernel, sizes), out_shape=(jax.ShapeDtyp...  61.2 us

profile of v2, /device:TPU:1, one launch (start us, length us, event | category | flops | bytes accessed | tf_op | source)
XLA Modules:
  0.0 63.0 jit_solution(1398397524709372881)
XLA Ops:
  0.6 61.2 %shard_map.174 = (bf16[1024,128]{1,0:T(8,128)(2,1)S(1)}, f32[1024,128]{1,0:T(8,128)S(1)}, f32[8,128,128]{2,1,0:T(8,128)S(1)}, f32[2,128]{1,0:T(2,128)S(1)}) custom-call(bf16[1024,128]{1,0:T(8,128)(2,1)} %refs_0_.1, bf16[1024,128]{1,0:T(8,128)(2,1)} %refs_1_.1, s32[16,1024]{1,0:T(8,128)} %bitcast.4, s32[4,64]{1,0:T(4,128)} %refs_3_.1, s32[1,1024]{1,0:T(1,128)} %bitcast.5, ...), custom_call_target="tpu_custom_call" | custom-call | tf_op jit(solution)/shard_map/pallas_call | solution.py:580
  61.8 1.1 %shard_map.175 = (bf16[1024,128]{1,0:T(8,128)(2,1)}, f32[1024,128]{1,0:T(8,128)}, f32[8,128,128]{2,1,0:T(8,128)}, f32[2,128]{1,0:T(2,128)}) custom-call(bf16[1024,128]{1,0:T(8,128)(2,1)S(1)} %get-tuple-element.8.refs_0_, f32[1024,128]{1,0:T(8,128)S(1)} %get-tuple-element.9.refs_1_, f32[8,128,128]{2,1,0:T(8,128)S(1)} %get-tuple-element.10.refs_2_, ...), custom_call_target="tpu_custom_call" | custom-call | tf_op jit(solution)/shard_map/pallas_call | solution.py:597

commit v3 on v2

--- a/solution.py
+++ b/solution.py
@@ -51,6 +51,19 @@
     up = 1.0 + t
     act = h * up
     return act, up + act * (1.0 - t)
+
+
+def narrow_half_silu(h):
+    h = h.astype(BF16)
+    t = jnp.tanh(h)
+    one = jnp.ones((), BF16)
+    up = one + t
+    act = h * up
+    return act, up + act * (one - t)
+
+
+def rows_of(row):
+    return jnp.concatenate([jnp.broadcast_to(row, (16, row.shape[1])).astype(BF16)] * (W // 16), axis=0)
 
 
 def centred_pair(w):
@@ -169,8 +182,8 @@
         remote(sbuf.at[pl.ds(q * W, W)], ghost.at[pl.ds(q * W, W)], halo_s.at[q], halo_r.at[q], halo_to[q])
         for q in range(4)
     ]
-    for c in halo:
-        c.start()
+    for q in (2, 3, 0, 1):
+        halo[q].start()
 
     eye = jnp.where(
         lax.broadcasted_iota(jnp.int32, (W, W), 0) == lax.broadcasted_iota(jnp.int32, (W, W), 1), 1.0, 0.0
@@ -256,10 +269,9 @@
                 lanes = slice(q * CHUNK, (q + 1) * CHUNK)
                 hot = jnp.concatenate([one_hot(local[c : c + 1, :], slot_id) for c in (2 * q, 2 * q + 1)], axis=1)
                 oh_all[t, :, lanes] = hot
-                act, slope = half_silu(mm(window, hot) + jnp.concatenate([recv_of[half]] * 2, axis=1))
-                act_b = act.astype(BF16)
+                act_b, slope = narrow_half_silu(mm(window, hot) + jnp.concatenate([recv_of[half]] * 2, axis=1))
                 act_all[t, :, lanes] = act_b
-                slope_all[t, :, lanes] = slope.astype(BF16)
+                slope_all[t, :, lanes] = slope
                 normed, inv = norm_centred(mm(we_c[...], twice(act_b)))
                 norm_all[t, :, lanes] = normed.astype(BF16)
                 inv_all[t, :, lanes] = inv
@@ -274,11 +286,11 @@
     halo[2].wait()
     halo[3].wait()
     ghost_tables(2 * W)
-    lax.fori_loop(0, PAIRS // 2, lambda k, c: forward((k // 2) * 4 + 2 + lax.rem(k, 2), c), 0)
+    lax.fori_loop(0, PAIRS // 4, lambda k, c: forward(k * 4 + 3, forward(k * 4 + 2, c)), 0)
     halo[0].wait()
     halo[1].wait()
     ghost_tables(0)
-    lax.fori_loop(0, PAIRS // 2, lambda k, c: forward((k // 2) * 4 + lax.rem(k, 2), c), 0)
+    lax.fori_loop(0, PAIRS // 4, lambda k, c: forward(k * 4 + 1, forward(k * 4, c)), 0)
 
     def node_forward(u, carry):
         at = pl.multiple_of(u * NODE, NODE)
@@ -296,7 +308,7 @@
     def widen(v):
         return jnp.concatenate([v] * (NODE // W), axis=1)
 
-    lax.fori_loop(0, ROWS // NODE, node_forward, 0)
+    lax.fori_loop(0, ROWS // NODE // 2, lambda k, c: node_forward(2 * k + 1, node_forward(2 * k, c)), 0)
 
     pf[gz] = nt(fine_t[...], oh_clus[...]).astype(BF16)
     pool_send(pf, pf_s, pf_r)
@@ -353,7 +365,7 @@
             total = total + v[:, b * W : (b + 1) * W]
         return total
 
-    lax.fori_loop(0, ROWS // NODE, node_back, 0)
+    lax.fori_loop(0, ROWS // NODE // 2, lambda k, c: node_back(2 * k + 1, node_back(2 * k, c)), 0)
 
     def put(buf, index, mat, width):
         per = W // c_rows
@@ -430,15 +442,17 @@
         back_of = []
         for half in range(2):
             t = 2 * u + half
-            gc = jnp.concatenate([gc_of[half]] * 2, axis=1)
+            gc = jnp.concatenate([gc_of[half].astype(BF16)] * 2, axis=1)
             total = None
             for q in range(STEPS):
                 lanes = slice(q * CHUNK, (q + 1) * CHUNK)
-                normed = norm_all[t, :, lanes].astype(F32)
-                gz_b = ((gc - normed * mean0(gc * normed)) * inv_all[t, :, lanes]).astype(BF16)
+                normed = norm_all[t, :, lanes]
+                shared = rows_of(mean0((gc * normed).astype(F32)))
+                gz_b = (gc - normed * shared) * rows_of(inv_all[t, :, lanes])
                 gz_tmp[half, :, lanes] = gz_b
-                gpre = mm(w_edge_h, gz_b) * slope_all[t, :, lanes].astype(F32)
-                gp_tmp[half, :, lanes] = gpre.astype(BF16)
+                gpre_b = mm(w_edge_h, gz_b).astype(BF16) * slope_all[t, :, lanes]
+                gp_tmp[half, :, lanes] = gpre_b
+                gpre = gpre_b.astype(F32)
                 part = gpre[:, :W] + gpre[:, W:]
                 total = part if total is None else total + part
             dw_edge[...] += nt(act_all[t], gz_tmp[half])
@@ -454,12 +468,19 @@
         remote(backbuf.at[pl.ds(q * W, W)], ret.at[pl.ds(q * W, W)], ret_s.at[q], ret_r.at[q], back_to[q])
         for q in range(4)
     ]
-    lax.fori_loop(0, PAIRS // 2, lambda k, c: backward((k // 2) * 4 + lax.rem(k, 2), c), 0)
+    lax.fori_loop(0, PAIRS // 4, lambda k, c: backward(k * 4 + 1, backward(k * 4, c)), 0)
     backbuf[: 2 * W, :] = gp_ghost[: 2 * W, :].astype(BF16)
     back[0].start()
     back[1].start()
-    reduce_mid(early, early_in, early_mid, e1s, e1r, e2s, e2r)
-    lax.fori_loop(0, PAIRS // 2, lambda k, c: backward((k // 2) * 4 + 2 + lax.rem(k, 2), c), 0)
+
+    def backward_near(k, c):
+        @pl.when(k == 1)
+        def _():
+            reduce_mid(early, early_in, early_mid, e1s, e1r, e2s, e2r)
+
+        return backward(k * 4 + 3, backward(k * 4 + 2, c))
+
+    lax.fori_loop(0, PAIRS // 4, backward_near, 0)
     backbuf[2 * W :, :] = gp_ghost[2 * W :, :].astype(BF16)
     back[2].start()
     back[3].start()
@@ -472,7 +493,6 @@
     put(late, 2, dw_edge[...], c_rows)
     put(late, 3, dw_pout, c_rows)
     reduce_out(late, late_in, l1s, l1r)
-    gather_out(early_mid, early_out, e2s, e2r, e3s, e3r)
 
     gfine_t[...] += (
         mm(w_self[...], gpn_t[...]) + mm(w_recv[...], grecv_t[...]) + nt(w_send[...], own_b)
@@ -483,6 +503,7 @@
     side_b = jnp.concatenate([ret[q * TILE : (q + 1) * TILE, :] for q in (6, 4, 7, 5)], axis=0)
     ret_t = (nt(w_send[...], side_a) + nt(w_send[...], side_b)).astype(BF16)
     gfine_t[...] += mm(ret_t, oh_send[...])
+    gather_out(early_mid, early_out, e2s, e2r, e3s, e3r)
     reduce_mid(late, late_in, late_mid, l1s, l1r, l2s, l2r)
     for b in range(PAIRS):
         grad_o[b * W : (b + 1) * W, :] = jnp.transpose(gfine_t[:, b * W : (b + 1) * W])
@@ -506,9 +527,12 @@
 
 
 def pass_on(*refs):
-    half = len(refs) // 2
-    for src, dst in zip(refs[:half], refs[half:]):
-        dst[...] = src[...]
+    sems = refs[-1]
+    copies = [pltpu.make_async_copy(a, b, sems.at[i]) for i, (a, b) in enumerate(zip(refs[:4], refs[4:8]))]
+    for c in copies:
+        c.start()
+    for c in copies:
+        c.wait()
 
 
 def solution(mesh):
@@ -598,7 +622,8 @@
             pass_on,
             out_shape=tuple(jax.ShapeDtypeStruct(r.shape, r.dtype) for r in results),
             in_specs=[pl.BlockSpec(memory_space=pltpu.VMEM)] * 4,
-            out_specs=tuple([pl.BlockSpec(memory_space=pltpu.VMEM)] * 4),
+            out_specs=tuple([pl.BlockSpec(memory_space=pltpu.HBM)] * 4),
+            scratch_shapes=[pltpu.SemaphoreType.DMA((4,))],
             compiler_params=pltpu.CompilerParams(vmem_limit_bytes=8 * 1024 * 1024),
         )(*results)
 

time: 63 us -> 57.2 us (0.908)
  Pallas kernels: 62.3 us -> 56.5 us
    pallas_call x1, Pallas kernels: 61.2 us -> 55.4 us  [step(): pl.pallas_call(functools.partial(kernel, sizes), out_shape=(jax.ShapeDtyp...]
where the time goes in v3:
time: 57.2 us; the launch traced here: 57.1 us
  Pallas kernels  56.5 us (99%)
  between operations  0.65 us (1%)
    pallas_call x1, Pallas kernels, step(): pl.pallas_call(functools.partial(kernel, sizes), out_shape=(jax.ShapeDtyp...  55.4 us

profile of v3, /device:TPU:1, one launch (start us, length us, event | category | flops | bytes accessed | tf_op | source)
XLA Modules:
  0.0 57.1 jit_solution(9648488033210627699)
XLA Ops:
  0.6 55.4 %shard_map.174 = (bf16[1024,128]{1,0:T(8,128)(2,1)S(1)}, f32[1024,128]{1,0:T(8,128)S(1)}, f32[8,128,128]{2,1,0:T(8,128)S(1)}, f32[2,128]{1,0:T(2,128)S(1)}) custom-call(bf16[1024,128]{1,0:T(8,128)(2,1)} %refs_0_.1, bf16[1024,128]{1,0:T(8,128)(2,1)} %refs_1_.1, s32[16,1024]{1,0:T(8,128)} %bitcast.4, s32[4,64]{1,0:T(4,128)} %refs_3_.1, s32[1,1024]{1,0:T(1,128)} %bitcast.5, ...), custom_call_target="tpu_custom_call" | custom-call | tf_op jit(solution)/shard_map/pallas_call | solution.py:604
  56.0 1.1 %shard_map.175 = (bf16[1024,128]{1,0:T(8,128)(2,1)}, f32[1024,128]{1,0:T(8,128)}, f32[8,128,128]{2,1,0:T(8,128)}, f32[2,128]{1,0:T(2,128)}) custom-call(bf16[1024,128]{1,0:T(8,128)(2,1)S(1)} %get-tuple-element.8.refs_0_, f32[1024,128]{1,0:T(8,128)S(1)} %get-tuple-element.9.refs_1_, f32[8,128,128]{2,1,0:T(8,128)S(1)} %get-tuple-element.10.refs_2_, ...), custom_call_target="tpu_custom_call" | custom-call | tf_op jit(solution)/shard_map/pallas_call | solution.py:621

commit v4 on v3

--- a/solution.py
+++ b/solution.py
@@ -73,6 +73,10 @@
     return jnp.concatenate([high, (centred - high.astype(F32)).astype(BF16)], axis=1)
 
 
+def beside(parts):
+    return jnp.concatenate(parts, axis=1)
+
+
 def twice(v):
     return jnp.concatenate([v, v], axis=0)
 
@@ -105,11 +109,15 @@
     (lat, gm, nb, send, clus, w_send, w_recv, w_edge, w_self, w_agg, w_node, w_pin, w_pout, egain, ngain) = near
     mixed_o, grad_o, mats_o, gains_o = refs[15:19]
     (sbuf, ghost, ret, backbuf, pg, pf, early, early_in, early_mid, early_out, late, late_in, late_mid, late_out,
-     lat_t, gm_t, oh_send, oh_clus, tab, tab_sh, gtab, gtab_sh, recv_t, wsa_t, we_c, wn_c,
+     lat_t, gm_t, oh_send, oh_clus, tab, tab_sh, gtab, gtab_sh, recv_t, wsa_t, we_c, wn_c, delta,
      oh_all, act_all, slope_all, norm_all, inv_all, sum_t, agg_t, an_t, nslope_t, nn_t, ninv_t, fine_t, gfine_t,
-     gy_t, gpn_t, gc_t, grecv_t, gz_tmp, gp_tmp, gp_own, gp_ghost, dw_edge, sums) = refs[19:68]
+     gy_t, gpn_t, gc_t, grecv_t, gp_own, gp_ghost, dw_edge, sums) = refs[19:67]
     (halo_s, halo_r, ret_s, ret_r, pg_s, pg_r, pf_s, pf_r,
-     e1s, e1r, e2s, e2r, e3s, e3r, l1s, l1r, l2s, l2r, l3s, l3r) = refs[68:-16]
+     e1s, e1r, e2s, e2r, e3s, e3r, l1s, l1r, l2s, l2r, l3s, l3r) = refs[67:-16]
+    loads = [pltpu.make_async_copy(a, b, in_sems.at[i]) for i, (a, b) in enumerate(zip(far, near))]
+    for i in (3, 0, 1, 4, *range(5, 15), 2):
+        loads[i].start()
+
     n_x, n_y, n_z = sizes
     n_a, n_b = n_x * n_z, n_y
     c_rows = 4 * W // n_a
@@ -118,24 +126,28 @@
     x_low = (lax.rem(gx + n_x - 1, n_x), gy, gz)
     y_up = (gx, lax.rem(gy + 1, n_y), gz)
     y_low = (gx, lax.rem(gy + n_y - 1, n_y), gz)
-    rank_a = ((gx // 2) * 2 + lax.rem(gy, 2)) * n_z + gz
-    rank_b = lax.rem(gx, 2) * (n_y // 2) + gy // 2
-
-    def z_peer(k):
-        return lax.rem(gz + k, n_z)
-
-    def a_peer(k):
-        return lax.rem(rank_a + k, n_a)
-
-    def a_dev(r):
-        yc = r // n_z
-        return ((yc // 2) * 2 + lax.rem(gx, 2), (gy // 2) * 2 + lax.rem(yc, 2), lax.rem(r, n_z))
-
-    def b_peer(k):
-        return lax.rem(rank_b + k, n_b)
-
-    def b_dev(r):
-        return ((gx // 2) * 2 + r // (n_y // 2), lax.rem(r, n_y // 2) * 2 + lax.rem(gy, 2), gz)
+    y_now, z_high = lax.div(gx, 2), lax.rem(gx, 2)
+    z_low, core = lax.div(gy, 2), lax.rem(gy, 2)
+    n_yc, n_zl = n_x // 2, n_y // 2
+    z_now = z_high * n_zl + z_low
+    rank_a, rank_b = (y_now * 2 + core) * n_z + gz, z_now
+
+    def hops(step, n):
+        return min(step, n - step)
+
+    ys = [lax.rem(y_now + d, n_yc) for d in range(n_yc)]
+    cs = [core, 1 - core]
+    xs = [lax.rem(gz + d, n_z) for d in range(n_z)]
+    order = sorted(
+        [(d, e, f) for d in range(n_yc) for e in range(2) for f in range(n_z)][1:],
+        key=lambda o: (-hops(o[0], n_yc) - hops(o[2], n_z), o),
+    )
+    plane = [
+        ((ys[d] * 2 + cs[e]) * n_z + xs[f], (ys[d] * 2 + z_high, z_low * 2 + cs[e], xs[f])) for d, e, f in order
+    ]
+    zs = [lax.rem(z_now + d, n_b) for d in sorted(range(1, n_b), key=lambda d: (-hops(d, n_b), d))]
+    column = [(z, (y_now * 2 + lax.div(z, n_zl), lax.rem(z, n_zl) * 2 + core, gz)) for z in zs]
+    row = [(xs[d], (gx, gy, xs[d])) for d in sorted(range(1, n_z), key=lambda d: (-hops(d, n_z), d))]
 
     def remote(src, dst, s, r, dev):
         return pltpu.make_async_remote_copy(
@@ -145,24 +157,9 @@
     def drain(ref, sem):
         pltpu.make_async_copy(ref, ref, sem).wait()
 
-    loads = [pltpu.make_async_copy(a, b, in_sems.at[i]) for i, (a, b) in enumerate(zip(far, near))]
-    for i in (3, 0, 1, 4, *range(5, 15), 2):
-        loads[i].start()
-
     barrier = pltpu.get_barrier_semaphore()
-    for dev in (x_up, x_low, y_up, y_low):
+    for dev in (x_up, x_low, y_up, y_low, *[d for _, d in plane], *[d for _, d in column]):
         pl.semaphore_signal(barrier, inc=1, device_id=dev, device_id_type=MESH)
-
-    def greet_a(k, c):
-        pl.semaphore_signal(barrier, inc=1, device_id=a_dev(a_peer(k)), device_id_type=MESH)
-        return c
-
-    def greet_b(k, c):
-        pl.semaphore_signal(barrier, inc=1, device_id=b_dev(b_peer(k)), device_id_type=MESH)
-        return c
-
-    lax.fori_loop(1, n_a, greet_a, 0)
-    lax.fori_loop(1, n_b, greet_b, 0)
 
     lane_row = lax.broadcasted_iota(jnp.int32, (TILE, W), 1)
     loads[3].wait()
@@ -196,28 +193,12 @@
     for b in range(PAIRS):
         oh_clus[:, b * W : (b + 1) * W] = one_hot(clus_f[:, b * W : (b + 1) * W], cl_id)
 
-    def pool_send(buf, sems_s, sems_r):
-        def go(k, c):
-            to = (gx, gy, z_peer(k))
-            remote(buf.at[gz], buf.at[gz], sems_s.at[k], sems_r.at[gz], to).start()
-            return c
-
-        lax.fori_loop(1, n_z, go, 0)
-
-    def pool_wait(buf, sems_s, sems_r):
-        def go(k, c):
-            src = lax.rem(gz + n_z - k, n_z)
-            remote(buf.at[gz], buf.at[src], sems_s.at[k], sems_r.at[src], (gx, gy, z_peer(k))).wait_recv()
-            return c
-
-        lax.fori_loop(1, n_z, go, 0)
-
-    def pool_done(buf, sems_s, sems_r):
-        def go(k, c):
-            remote(buf.at[gz], buf.at[gz], sems_s.at[k], sems_r.at[gz], (gx, gy, z_peer(k))).wait_send()
-            return c
-
-        lax.fori_loop(1, n_z, go, 0)
+    def pool_send(buf, s, r):
+        for _, dev in row:
+            remote(buf.at[gz], buf.at[gz], s, r, dev).start()
+
+    def pool_wait(buf, r):
+        drain(buf.at[pl.ds(0, n_z - 1)], r)
 
     pg[gz] = nt(gm_t[...], oh_clus[...]).astype(BF16)
     pool_send(pg, pg_s, pg_r)
@@ -314,13 +295,13 @@
     pool_send(pf, pf_s, pf_r)
     wpin_t = jnp.transpose(w_pin[...].astype(F32)).astype(BF16)
     wpout_t = jnp.transpose(w_pout[...].astype(F32)).astype(BF16)
-    pool_wait(pg, pg_s, pg_r)
+    pool_wait(pg, pg_r)
     gd = pg[0].astype(F32)
     for k in range(1, n_z):
         gd = gd + pg[k].astype(F32)
     gd_b = gd.astype(BF16)
     gac = mm(w_pout[...], gd_b)
-    pool_wait(pf, pf_s, pf_r)
+    pool_wait(pf, pf_r)
     pooled = pf[0].astype(F32)
     for k in range(1, n_z):
         pooled = pooled + pf[k].astype(F32)
@@ -332,7 +313,7 @@
     delta_b = mm(wpout_t, ac_b).astype(BF16)
     gpc_b = (gac * (s + ac * (1.0 - s))).astype(BF16)
     gpool_b = mm(w_pin[...], gpc_b).astype(BF16)
-    both = jnp.concatenate([delta_b, gpool_b], axis=0)
+    delta[...] = delta_b
     dw_pin = nt(pooled_b, gpc_b) * (1.0 / n_z)
     dw_pout = nt(ac_b, gd_b) * (1.0 / n_z)
 
@@ -340,11 +321,7 @@
 
     def node_back(u, carry):
         at = pl.multiple_of(u * NODE, NODE)
-        added = mm(both, oh_clus[:, pl.ds(at, NODE)])
-        mixed = fine_t[:, pl.ds(at, NODE)].astype(F32) + added[:W, :]
-        for b in range(NODE // W):
-            mixed_o[pl.ds(at + b * W, W), :] = jnp.transpose(mixed[:, b * W : (b + 1) * W]).astype(BF16)
-        gf = gm_t[:, pl.ds(at, NODE)].astype(F32) + added[W:, :]
+        gf = gm_t[:, pl.ds(at, NODE)].astype(F32) + mm(gpool_b, oh_clus[:, pl.ds(at, NODE)])
         gfine_t[:, pl.ds(at, NODE)] = gf
         nn = nn_t[:, pl.ds(at, NODE)]
         sums[1] += narrow(gf * nn)
@@ -374,12 +351,8 @@
     def reduce_out(buf, into, s, r):
         into[rank_a] = buf[rank_a]
 
-        def go(k, c):
-            to = a_peer(k)
-            remote(buf.at[to], into.at[rank_a], s, r, a_dev(to)).start()
-            return c
-
-        lax.fori_loop(1, n_a, go, 0)
+        for to, dev in plane:
+            remote(buf.at[to], into.at[rank_a], s, r, dev).start()
 
     def reduce_mid(buf, into, mid, s, r, s2, r2):
         drain(into.at[pl.ds(0, n_a - 1)], r)
@@ -387,12 +360,8 @@
         for k in range(1, n_a):
             total = total + into[k].astype(F32)
         mid[rank_b] = total.astype(BF16)
-
-        def go(k, c):
-            remote(mid.at[rank_b], mid.at[rank_b], s2, r2, b_dev(b_peer(k))).start()
-            return c
-
-        lax.fori_loop(1, n_b, go, 0)
+        for _, dev in column:
+            remote(mid.at[rank_b], mid.at[rank_b], s2, r2, dev).start()
 
     def gather_out(mid, out, s2, r2, s3, r3):
         drain(mid.at[pl.ds(0, n_b - 1)], r2)
@@ -400,12 +369,8 @@
         for k in range(1, n_b):
             total = total + mid[k].astype(F32)
         out[rank_a] = total.astype(BF16)
-
-        def go(k, c):
-            remote(out.at[rank_a], out.at[rank_a], s3, r3, a_dev(a_peer(k))).start()
-            return c
-
-        lax.fori_loop(1, n_a, go, 0)
+        for _, dev in plane:
+            remote(out.at[rank_a], out.at[rank_a], s3, r3, dev).start()
 
     def finish(buf, mid, out, s, s2, s3, r3):
         drain(out.at[pl.ds(0, n_a - 1)], r3)
@@ -442,6 +407,7 @@
         back_of = []
         for half in range(2):
             t = 2 * u + half
+            gzs, gps = [], []
             gc = jnp.concatenate([gc_of[half].astype(BF16)] * 2, axis=1)
             total = None
             for q in range(STEPS):
@@ -449,14 +415,14 @@
                 normed = norm_all[t, :, lanes]
                 shared = rows_of(mean0((gc * normed).astype(F32)))
                 gz_b = (gc - normed * shared) * rows_of(inv_all[t, :, lanes])
-                gz_tmp[half, :, lanes] = gz_b
+                gzs.append(gz_b)
                 gpre_b = mm(w_edge_h, gz_b).astype(BF16) * slope_all[t, :, lanes]
-                gp_tmp[half, :, lanes] = gpre_b
+                gps.append(gpre_b)
                 gpre = gpre_b.astype(F32)
                 part = gpre[:, :W] + gpre[:, W:]
                 total = part if total is None else total + part
-            dw_edge[...] += nt(act_all[t], gz_tmp[half])
-            window = nt(oh_all[t], gp_tmp[half])
+            dw_edge[...] += nt(act_all[t], beside(gzs))
+            window = nt(oh_all[t], beside(gps))
             gp_own[pl.ds(at + half * TILE, W), :] += window[:W, :]
             gp_ghost[pl.ds(at_g + half * TILE, TILE), :] += window[W:, :]
             back_of.append(total + swap(total))
@@ -504,6 +470,9 @@
     ret_t = (nt(w_send[...], side_a) + nt(w_send[...], side_b)).astype(BF16)
     gfine_t[...] += mm(ret_t, oh_send[...])
     gather_out(early_mid, early_out, e2s, e2r, e3s, e3r)
+    mixed = fine_t[...].astype(F32) + mm(delta[...], oh_clus[...])
+    for b in range(PAIRS):
+        mixed_o[b * W : (b + 1) * W, :] = jnp.transpose(mixed[:, b * W : (b + 1) * W]).astype(BF16)
     reduce_mid(late, late_in, late_mid, l1s, l1r, l2s, l2r)
     for b in range(PAIRS):
         grad_o[b * W : (b + 1) * W, :] = jnp.transpose(gfine_t[:, b * W : (b + 1) * W])
@@ -518,8 +487,8 @@
         emit(early_out, index, place)
     scale = float(ROWS * n_x * n_y * n_z) ** (-0.5)
     gains_o[...] = early_out[0, c_rows : c_rows + 2, :].astype(F32) * scale
-    pool_done(pg, pg_s, pg_r)
-    pool_done(pf, pf_s, pf_r)
+    pool_wait(pg, pg_s)
+    pool_wait(pf, pf_s)
     gather_out(late_mid, late_out, l2s, l2r, l3s, l3r)
     finish(late, late_mid, late_out, l1s, l2s, l3s, l3r)
     for index, place in enumerate((0, 1, 2, 7)):
@@ -568,6 +537,7 @@
         v((W, 2 * W), BF16),
         v((W, 2 * W), BF16),
         v((W, 2 * W), BF16),
+        v((W, CLUSTERS), BF16),
         v((tiles, SLOTS, edges), BF16),
         v((tiles, W, edges), BF16),
         v((tiles, W, edges), BF16),
@@ -585,15 +555,12 @@
         v((W, ROWS), BF16),
         v((W, ROWS), F32),
         v((W, ROWS), BF16),
-        v((2, W, edges), BF16),
-        v((2, W, edges), BF16),
         v((ROWS + TILE, W), F32),
         v((GHOSTS, W), F32),
         v((W, W), F32),
         v((2, W, W), F32),
         dma((4,)), dma((4,)), dma((4,)), dma((4,)),
-        dma((n_z,)), dma((n_z,)), dma((n_z,)), dma((n_z,)),
-        *[dma for _ in range(12)],
+        *[dma for _ in range(16)],
         v((ROWS, W), BF16), v((ROWS, W), BF16), v((NEIGH, ROWS), jnp.int32), v((4, TILE), jnp.int32),
         v((1, ROWS), jnp.int32), *[v((W, W), BF16) for _ in range(8)], v((1, W), F32), v((1, W), F32),
         dma((15,)),

time: 57.2 us -> 54.8 us (0.958)
  Pallas kernels: 56.5 us -> 54.1 us
    pallas_call x1, Pallas kernels: 55.4 us -> 53 us  [step(): pl.pallas_call(functools.partial(kernel, sizes), out_shape=(jax.ShapeDtyp...]
where the time goes in v4:
time: 54.8 us; the launch traced here: 54.7 us
  Pallas kernels  54.1 us (99%)
  between operations  0.65 us (1%)
    pallas_call x1, Pallas kernels, step(): pl.pallas_call(functools.partial(kernel, sizes), out_shape=(jax.ShapeDtyp...  53 us

profile of v4, /device:TPU:1, one launch (start us, length us, event | category | flops | bytes accessed | tf_op | source)
XLA Modules:
  0.0 54.7 jit_solution(6033524382278786034)
XLA Ops:
  0.6 53.0 %shard_map.174 = (bf16[1024,128]{1,0:T(8,128)(2,1)S(1)}, f32[1024,128]{1,0:T(8,128)S(1)}, f32[8,128,128]{2,1,0:T(8,128)S(1)}, f32[2,128]{1,0:T(2,128)S(1)}) custom-call(bf16[1024,128]{1,0:T(8,128)(2,1)} %refs_0_.1, bf16[1024,128]{1,0:T(8,128)(2,1)} %refs_1_.1, s32[16,1024]{1,0:T(8,128)} %bitcast.4, s32[4,64]{1,0:T(4,128)} %refs_3_.1, s32[1,1024]{1,0:T(1,128)} %bitcast.5, ...), custom_call_target="tpu_custom_call" | custom-call | tf_op jit(solution)/shard_map/pallas_call | solution.py:571
  53.6 1.1 %shard_map.175 = (bf16[1024,128]{1,0:T(8,128)(2,1)}, f32[1024,128]{1,0:T(8,128)}, f32[8,128,128]{2,1,0:T(8,128)}, f32[2,128]{1,0:T(2,128)}) custom-call(bf16[1024,128]{1,0:T(8,128)(2,1)S(1)} %get-tuple-element.8.refs_0_, f32[1024,128]{1,0:T(8,128)S(1)} %get-tuple-element.9.refs_1_, f32[8,128,128]{2,1,0:T(8,128)S(1)} %get-tuple-element.10.refs_2_, ...), custom_call_target="tpu_custom_call" | custom-call | tf_op jit(solution)/shard_map/pallas_call | solution.py:588

commit v5 on v4

--- a/solution.py
+++ b/solution.py
@@ -57,9 +57,7 @@
     h = h.astype(BF16)
     t = jnp.tanh(h)
     one = jnp.ones((), BF16)
-    up = one + t
-    act = h * up
-    return act, up + act * (one - t)
+    return h * (one + t), t
 
 
 def rows_of(row):
@@ -77,6 +75,10 @@
     return jnp.concatenate(parts, axis=1)
 
 
+def beside(parts):
+    return jnp.concatenate(parts, axis=1)
+
+
 def twice(v):
     return jnp.concatenate([v, v], axis=0)
 
@@ -109,11 +111,11 @@
     (lat, gm, nb, send, clus, w_send, w_recv, w_edge, w_self, w_agg, w_node, w_pin, w_pout, egain, ngain) = near
     mixed_o, grad_o, mats_o, gains_o = refs[15:19]
     (sbuf, ghost, ret, backbuf, pg, pf, early, early_in, early_mid, early_out, late, late_in, late_mid, late_out,
-     lat_t, gm_t, oh_send, oh_clus, tab, tab_sh, gtab, gtab_sh, recv_t, wsa_t, we_c, wn_c, delta,
-     oh_all, act_all, slope_all, norm_all, inv_all, sum_t, agg_t, an_t, nslope_t, nn_t, ninv_t, fine_t, gfine_t,
-     gy_t, gpn_t, gc_t, grecv_t, gp_own, gp_ghost, dw_edge, sums) = refs[19:67]
+     lat_t, gm_t, oh_send, oh_clus, tab, tab_sh, gtab, gtab_sh, recv_t, wsa_t, we_c, wn_c, delta, ghost_t,
+     oh_all, act_cols, act_all, slope_all, norm_all, inv_all, sum_t, agg_t, an_t, nslope_t, nn_t, ninv_t, fine_t, gfine_t,
+     gy_t, gpn_t, gc_t, grecv_t, gp_own, gp_ghost, dw_edge, sums) = refs[19:69]
     (halo_s, halo_r, ret_s, ret_r, pg_s, pg_r, pf_s, pf_r,
-     e1s, e1r, e2s, e2r, e3s, e3r, l1s, l1r, l2s, l2r, l3s, l3r) = refs[67:-16]
+     e1s, e1r, e2s, e2r, e3s, e3r, l1s, l1r, l2s, l2r, l3s, l3r) = refs[69:-16]
     loads = [pltpu.make_async_copy(a, b, in_sems.at[i]) for i, (a, b) in enumerate(zip(far, near))]
     for i in (3, 0, 1, 4, *range(5, 15), 2):
         loads[i].start()
@@ -227,32 +229,40 @@
         gtab[:, part] = nt(wsend_t, own).astype(BF16)
         gtab_sh[:, part] = nt(wsend_t, jnp.concatenate([own[TILE:, :], own[:TILE, :]], axis=0)).astype(BF16)
 
-    def forward(u, carry):
-        low = low_half()
+    def pick_tables(u, carry):
+        low8 = low_half()[:8, :]
         slot_id = lax.broadcasted_iota(jnp.int32, (SLOTS, W), 0).astype(F32).astype(BF16)
-        at = pl.multiple_of(u * W, W)
-        at_g = pl.multiple_of(lax.rem(u, GHOSTS // W) * W, W)
-        picks = nb[:, pl.ds(at, W)]
-        low8 = low[:8, :]
+        picks = nb[:, pl.ds(pl.multiple_of(u * W, W), W)]
         first, second = picks[:8, :], picks[8:, :]
         picks_of = (jnp.where(low8, first, swap(second)), jnp.where(low8, swap(first), second))
-        recv_of = spread_halves(recv_t[:, pl.ds(at, W)], low)
-        sums_of = []
         for half in range(2):
             t = 2 * u + half
             chosen = picks_of[half]
             local = jnp.where(chosen >= ROWS, (chosen & (TILE - 1)) + 2 * TILE, (chosen - t * TILE) & (ROWS - 1))
             local = local.astype(F32)
+            for q in range(STEPS):
+                for c in (2 * q, 2 * q + 1):
+                    oh_all[t, c] = one_hot(local[c : c + 1, :], slot_id)
+        return carry
+
+    lax.fori_loop(0, PAIRS, pick_tables, 0)
+
+    def forward(u, carry):
+        low = low_half()
+        at = pl.multiple_of(u * W, W)
+        at_g = pl.multiple_of(lax.rem(u, GHOSTS // W) * W, W)
+        recv_of = spread_halves(recv_t[:, pl.ds(at, W)], low)
+        sums_of = []
+        for half in range(2):
+            t = 2 * u + half
             own, far = (tab, gtab) if half == 0 else (tab_sh, gtab_sh)
             window = jnp.concatenate([own[:, pl.ds(at, W)], far[:, pl.ds(at_g, TILE)]], axis=1)
             total = None
             for q in range(STEPS):
                 lanes = slice(q * CHUNK, (q + 1) * CHUNK)
-                hot = jnp.concatenate([one_hot(local[c : c + 1, :], slot_id) for c in (2 * q, 2 * q + 1)], axis=1)
-                oh_all[t, :, lanes] = hot
-                act_b, slope = narrow_half_silu(mm(window, hot) + jnp.concatenate([recv_of[half]] * 2, axis=1))
+                act_b, bend = narrow_half_silu(mm(window, beside([oh_all[t, 2 * q], oh_all[t, 2 * q + 1]])) + jnp.concatenate([recv_of[half]] * 2, axis=1))
                 act_all[t, :, lanes] = act_b
-                slope_all[t, :, lanes] = slope
+                slope_all[t, :, lanes] = bend
                 normed, inv = norm_centred(mm(we_c[...], twice(act_b)))
                 norm_all[t, :, lanes] = normed.astype(BF16)
                 inv_all[t, :, lanes] = inv
@@ -274,7 +284,7 @@
     lax.fori_loop(0, PAIRS // 4, lambda k, c: forward(k * 4 + 1, forward(k * 4, c)), 0)
 
     def node_forward(u, carry):
-        at = pl.multiple_of(u * NODE, NODE)
+        at = u * NODE
         lat_b = lat_t[:, pl.ds(at, NODE)]
         an, slope = half_silu(mm(wsa_t[...], jnp.concatenate([lat_b, agg_t[:, pl.ds(at, NODE)]], axis=0)))
         an_b = an.astype(BF16)
@@ -289,10 +299,26 @@
     def widen(v):
         return jnp.concatenate([v] * (NODE // W), axis=1)
 
-    lax.fori_loop(0, ROWS // NODE // 2, lambda k, c: node_forward(2 * k + 1, node_forward(2 * k, c)), 0)
+    for k in range(ROWS // NODE):
+        node_forward(k, 0)
 
     pf[gz] = nt(fine_t[...], oh_clus[...]).astype(BF16)
     pool_send(pf, pf_s, pf_r)
+    ghost_t[...] = nt(eye, ghost[...]).astype(BF16)
+
+    def prepare(u, carry):
+        one = jnp.ones((), BF16)
+        for half in range(2):
+            t = 2 * u + half
+            for q in range(STEPS):
+                lanes = slice(q * CHUNK, (q + 1) * CHUNK)
+                bend, act = slope_all[t, :, lanes], act_all[t, :, lanes]
+                slope_all[t, :, lanes] = (one + bend) + act * (one - bend)
+                for i in range(CHUNK // W):
+                    act_cols[t, 2 * q + i] = act[:, i * W : (i + 1) * W]
+        return carry
+
+    lax.fori_loop(0, PAIRS, prepare, 0)
     wpin_t = jnp.transpose(w_pin[...].astype(F32)).astype(BF16)
     wpout_t = jnp.transpose(w_pout[...].astype(F32)).astype(BF16)
     pool_wait(pg, pg_r)
@@ -320,7 +346,7 @@
     sums[...] = jnp.zeros_like(sums)
 
     def node_back(u, carry):
-        at = pl.multiple_of(u * NODE, NODE)
+        at = u * NODE
         gf = gm_t[:, pl.ds(at, NODE)].astype(F32) + mm(gpool_b, oh_clus[:, pl.ds(at, NODE)])
         gfine_t[:, pl.ds(at, NODE)] = gf
         nn = nn_t[:, pl.ds(at, NODE)]
@@ -342,7 +368,8 @@
             total = total + v[:, b * W : (b + 1) * W]
         return total
 
-    lax.fori_loop(0, ROWS // NODE // 2, lambda k, c: node_back(2 * k + 1, node_back(2 * k, c)), 0)
+    for k in range(ROWS // NODE):
+        node_back(k, 0)
 
     def put(buf, index, mat, width):
         per = W // c_rows
@@ -421,8 +448,8 @@
                 gpre = gpre_b.astype(F32)
                 part = gpre[:, :W] + gpre[:, W:]
                 total = part if total is None else total + part
-            dw_edge[...] += nt(act_all[t], beside(gzs))
-            window = nt(oh_all[t], beside(gps))
+            dw_edge[...] += nt(beside([act_cols[t, c] for c in range(2 * STEPS)]), beside(gzs))
+            window = nt(beside([oh_all[t, c] for c in range(2 * STEPS)]), beside(gps))
             gp_own[pl.ds(at + half * TILE, W), :] += window[:W, :]
             gp_ghost[pl.ds(at_g + half * TILE, TILE), :] += window[W:, :]
             back_of.append(total + swap(total))
@@ -440,10 +467,6 @@
     back[1].start()
 
     def backward_near(k, c):
-        @pl.when(k == 1)
-        def _():
-            reduce_mid(early, early_in, early_mid, e1s, e1r, e2s, e2r)
-
         return backward(k * 4 + 3, backward(k * 4 + 2, c))
 
     lax.fori_loop(0, PAIRS // 4, backward_near, 0)
@@ -453,12 +476,12 @@
 
     gp_own[:TILE, :] += gp_own[ROWS:, :]
     own_b = gp_own[:ROWS, :].astype(BF16)
-    ghost_t = nt(eye, ghost[...]).astype(BF16)
-    put(late, 0, mm(lat_t[...], own_b) + mm(ghost_t, backbuf[...]), c_rows)
+    put(late, 0, mm(lat_t[...], own_b) + mm(ghost_t[...], backbuf[...]), c_rows)
     put(late, 1, nt(lat_t[...], grecv_t[...]), c_rows)
     put(late, 2, dw_edge[...], c_rows)
     put(late, 3, dw_pout, c_rows)
     reduce_out(late, late_in, l1s, l1r)
+    reduce_mid(early, early_in, early_mid, e1s, e1r, e2s, e2r)
 
     gfine_t[...] += (
         mm(w_self[...], gpn_t[...]) + mm(w_recv[...], grecv_t[...]) + nt(w_send[...], own_b)
@@ -469,11 +492,11 @@
     side_b = jnp.concatenate([ret[q * TILE : (q + 1) * TILE, :] for q in (6, 4, 7, 5)], axis=0)
     ret_t = (nt(w_send[...], side_a) + nt(w_send[...], side_b)).astype(BF16)
     gfine_t[...] += mm(ret_t, oh_send[...])
-    gather_out(early_mid, early_out, e2s, e2r, e3s, e3r)
     mixed = fine_t[...].astype(F32) + mm(delta[...], oh_clus[...])
     for b in range(PAIRS):
         mixed_o[b * W : (b + 1) * W, :] = jnp.transpose(mixed[:, b * W : (b + 1) * W]).astype(BF16)
     reduce_mid(late, late_in, late_mid, l1s, l1r, l2s, l2r)
+    gather_out(early_mid, early_out, e2s, e2r, e3s, e3r)
     for b in range(PAIRS):
         grad_o[b * W : (b + 1) * W, :] = jnp.transpose(gfine_t[:, b * W : (b + 1) * W])
 
@@ -538,7 +561,9 @@
         v((W, 2 * W), BF16),
         v((W, 2 * W), BF16),
         v((W, CLUSTERS), BF16),
-        v((tiles, SLOTS, edges), BF16),
+        v((W, GHOSTS), BF16),
+        v((tiles, edges // W, SLOTS, W), BF16),
+        v((tiles, edges // W, W, W), BF16),
         v((tiles, W, edges), BF16),
         v((tiles, W, edges), BF16),
         v((tiles, W, edges), BF16),

time: 54.8 us -> 52.8 us (0.964)
  Pallas kernels: 54.1 us -> 52 us
    pallas_call x1, Pallas kernels: 53 us -> 51 us  [step(): pl.pallas_call(functools.partial(kernel, sizes), out_shape=(jax.ShapeDtyp...]
where the time goes in v5:
time: 52.8 us; the launch traced here: 52.7 us
  Pallas kernels  52 us (98%)
  between operations  0.65 us (1%)
    pallas_call x1, Pallas kernels, step(): pl.pallas_call(functools.partial(kernel, sizes), out_shape=(jax.ShapeDtyp...  51 us
    pallas_call x1, Pallas kernels, step(): pl.pallas_call(pass_on, out_shape=tuple((jax.ShapeDtypeStruct(r.shape, r....  1.09 us

profile of v5, /device:TPU:1, one launch (start us, length us, event | category | flops | bytes accessed | tf_op | source)
XLA Modules:
  0.0 52.7 jit_solution(245892835984776781)
XLA Ops:
  0.6 51.0 %shard_map.174 = (bf16[1024,128]{1,0:T(8,128)(2,1)S(1)}, f32[1024,128]{1,0:T(8,128)S(1)}, f32[8,128,128]{2,1,0:T(8,128)S(1)}, f32[2,128]{1,0:T(2,128)S(1)}) custom-call(bf16[1024,128]{1,0:T(8,128)(2,1)} %refs_0_.1, bf16[1024,128]{1,0:T(8,128)(2,1)} %refs_1_.1, s32[16,1024]{1,0:T(8,128)} %bitcast.4, s32[4,64]{1,0:T(4,128)} %refs_3_.1, s32[1,1024]{1,0:T(1,128)} %bitcast.5, ...), custom_call_target="tpu_custom_call" | custom-call | tf_op jit(solution)/shard_map/pallas_call | solution.py:596
  51.6 1.1 %shard_map.175 = (bf16[1024,128]{1,0:T(8,128)(2,1)}, f32[1024,128]{1,0:T(8,128)}, f32[8,128,128]{2,1,0:T(8,128)}, f32[2,128]{1,0:T(2,128)}) custom-call(bf16[1024,128]{1,0:T(8,128)(2,1)S(1)} %get-tuple-element.8.refs_0_, f32[1024,128]{1,0:T(8,128)S(1)} %get-tuple-element.9.refs_1_, f32[8,128,128]{2,1,0:T(8,128)S(1)} %get-tuple-element.10.refs_2_, ...), custom_call_target="tpu_custom_call" | custom-call | tf_op jit(solution)/shard_map/pallas_call | solution.py:613

commit v6 on v5

--- a/solution.py
+++ b/solution.py
@@ -249,8 +249,8 @@
 
     def forward(u, carry):
         low = low_half()
-        at = pl.multiple_of(u * W, W)
-        at_g = pl.multiple_of(lax.rem(u, GHOSTS // W) * W, W)
+        at = u * W if isinstance(u, int) else pl.multiple_of(u * W, W)
+        at_g = u % (GHOSTS // W) * W if isinstance(u, int) else pl.multiple_of(lax.rem(u, GHOSTS // W) * W, W)
         recv_of = spread_halves(recv_t[:, pl.ds(at, W)], low)
         sums_of = []
         for half in range(2):
@@ -277,11 +277,13 @@
     halo[2].wait()
     halo[3].wait()
     ghost_tables(2 * W)
-    lax.fori_loop(0, PAIRS // 4, lambda k, c: forward(k * 4 + 3, forward(k * 4 + 2, c)), 0)
+    for u in (2, 3, 6, 7):
+        forward(u, 0)
     halo[0].wait()
     halo[1].wait()
     ghost_tables(0)
-    lax.fori_loop(0, PAIRS // 4, lambda k, c: forward(k * 4 + 1, forward(k * 4, c)), 0)
+    for u in (0, 1, 4, 5):
+        forward(u, 0)
 
     def node_forward(u, carry):
         at = u * NODE
@@ -428,8 +430,8 @@
 
     def backward(u, carry):
         low = low_half()
-        at = pl.multiple_of(u * W, W)
-        at_g = pl.multiple_of(lax.rem(u, GHOSTS // W) * W, W)
+        at = u * W if isinstance(u, int) else pl.multiple_of(u * W, W)
+        at_g = u % (GHOSTS // W) * W if isinstance(u, int) else pl.multiple_of(lax.rem(u, GHOSTS // W) * W, W)
         gc_of = spread_halves(gc_t[:, pl.ds(at, W)], low)
         back_of = []
         for half in range(2):
@@ -461,7 +463,8 @@
         remote(backbuf.at[pl.ds(q * W, W)], ret.at[pl.ds(q * W, W)], ret_s.at[q], ret_r.at[q], back_to[q])
         for q in range(4)
     ]
-    lax.fori_loop(0, PAIRS // 4, lambda k, c: backward(k * 4 + 1, backward(k * 4, c)), 0)
+    for u in (0, 1, 4, 5):
+        backward(u, 0)
     backbuf[: 2 * W, :] = gp_ghost[: 2 * W, :].astype(BF16)
     back[0].start()
     back[1].start()
@@ -469,7 +472,8 @@
     def backward_near(k, c):
         return backward(k * 4 + 3, backward(k * 4 + 2, c))
 
-    lax.fori_loop(0, PAIRS // 4, backward_near, 0)
+    for u in (2, 3, 6, 7):
+        backward(u, 0)
     backbuf[2 * W :, :] = gp_ghost[2 * W :, :].astype(BF16)
     back[2].start()
     back[3].start()

time: 52.8 us -> 51.9 us (0.983)
  Pallas kernels: 52 us -> 51 us
    pallas_call x1, Pallas kernels: 51 us -> 49.9 us  [step(): pl.pallas_call(functools.partial(kernel, sizes), out_shape=(jax.ShapeDtyp...]
where the time goes in v6:
time: 51.9 us; the launch traced here: 51.8 us
  Pallas kernels  51 us (98%)
  between operations  0.81 us (2%)
    pallas_call x1, Pallas kernels, step(): pl.pallas_call(functools.partial(kernel, sizes), out_shape=(jax.ShapeDtyp...  49.9 us
    pallas_call x1, Pallas kernels, step(): pl.pallas_call(pass_on, out_shape=tuple((jax.ShapeDtypeStruct(r.shape, r....  1.09 us

profile of v6, /device:TPU:1, one launch (start us, length us, event | category | flops | bytes accessed | tf_op | source)
XLA Modules:
  0.0 51.8 jit_solution(2074568426752937146)
XLA Ops:
  0.6 49.9 %shard_map.174 = (bf16[1024,128]{1,0:T(8,128)(2,1)S(1)}, f32[1024,128]{1,0:T(8,128)S(1)}, f32[8,128,128]{2,1,0:T(8,128)S(1)}, f32[2,128]{1,0:T(2,128)S(1)}) custom-call(bf16[1024,128]{1,0:T(8,128)(2,1)} %refs_0_.1, bf16[1024,128]{1,0:T(8,128)(2,1)} %refs_1_.1, s32[16,1024]{1,0:T(8,128)} %bitcast.4, s32[4,64]{1,0:T(4,128)} %refs_3_.1, s32[1,1024]{1,0:T(1,128)} %bitcast.5, ...), custom_call_target="tpu_custom_call" | custom-call | tf_op jit(solution)/shard_map/pallas_call | solution.py:600
  50.5 1.1 %shard_map.175 = (bf16[1024,128]{1,0:T(8,128)(2,1)}, f32[1024,128]{1,0:T(8,128)}, f32[8,128,128]{2,1,0:T(8,128)}, f32[2,128]{1,0:T(2,128)}) custom-call(bf16[1024,128]{1,0:T(8,128)(2,1)S(1)} %get-tuple-element.8.refs_0_, f32[1024,128]{1,0:T(8,128)S(1)} %get-tuple-element.9.refs_1_, f32[8,128,128]{2,1,0:T(8,128)S(1)} %get-tuple-element.10.refs_2_, ...), custom_call_target="tpu_custom_call" | custom-call | tf_op jit(solution)/shard_map/pallas_call | solution.py:617

commit v7 on v6

--- a/solution.py
+++ b/solution.py
@@ -19,7 +19,7 @@
 CHUNK = 256
 STEPS = TILE * NEIGH // CHUNK
 NODE = 256
-GAIN_ROWS = 16
+GAIN_ROWS = 8
 F32 = jnp.float32
 BF16 = jnp.bfloat16
 MESH = pl.DeviceIdType.MESH
@@ -181,8 +181,8 @@
         remote(sbuf.at[pl.ds(q * W, W)], ghost.at[pl.ds(q * W, W)], halo_s.at[q], halo_r.at[q], halo_to[q])
         for q in range(4)
     ]
-    for q in (2, 3, 0, 1):
-        halo[q].start()
+    for c in halo:
+        c.start()
 
     eye = jnp.where(
         lax.broadcasted_iota(jnp.int32, (W, W), 0) == lax.broadcasted_iota(jnp.int32, (W, W), 1), 1.0, 0.0
@@ -274,17 +274,6 @@
         agg_t[:, pl.ds(at, W)] = (total * eg).astype(BF16)
         return carry
 
-    halo[2].wait()
-    halo[3].wait()
-    ghost_tables(2 * W)
-    for u in (2, 3, 6, 7):
-        forward(u, 0)
-    halo[0].wait()
-    halo[1].wait()
-    ghost_tables(0)
-    for u in (0, 1, 4, 5):
-        forward(u, 0)
-
     def node_forward(u, carry):
         at = u * NODE
         lat_b = lat_t[:, pl.ds(at, NODE)]
@@ -301,7 +290,20 @@
     def widen(v):
         return jnp.concatenate([v] * (NODE // W), axis=1)
 
-    for k in range(ROWS // NODE):
+    halo[2].wait()
+    halo[3].wait()
+    ghost_tables(2 * W)
+    for u in (2, 3, 6, 7):
+        forward(u, 0)
+    for k in (1, 3):
+        node_forward(k, 0)
+    halo[0].wait()
+    halo[1].wait()
+    ghost_tables(0)
+    for u in (0, 1, 4, 5):
+        forward(u, 0)
+
+    for k in (0, 2):
         node_forward(k, 0)
 
     pf[gz] = nt(fine_t[...], oh_clus[...]).astype(BF16)
@@ -485,11 +487,11 @@
     put(late, 2, dw_edge[...], c_rows)
     put(late, 3, dw_pout, c_rows)
     reduce_out(late, late_in, l1s, l1r)
-    reduce_mid(early, early_in, early_mid, e1s, e1r, e2s, e2r)
 
     gfine_t[...] += (
         mm(w_self[...], gpn_t[...]) + mm(w_recv[...], grecv_t[...]) + nt(w_send[...], own_b)
     )
+    reduce_mid(early, early_in, early_mid, e1s, e1r, e2s, e2r)
     for c in back:
         c.wait()
     side_a = jnp.concatenate([ret[q * TILE : (q + 1) * TILE, :] for q in (2, 3, 0, 1)], axis=0)

time: 51.9 us -> 51.6 us (level)
  no operation moved by 1% of the time
where the time goes in v7:
time: 51.6 us; the launch traced here: 51.5 us
  Pallas kernels  50.7 us (98%)
  between operations  0.81 us (2%)
    pallas_call x1, Pallas kernels, step(): pl.pallas_call(functools.partial(kernel, sizes), out_shape=(jax.ShapeDtyp...  49.7 us
    pallas_call x1, Pallas kernels, step(): pl.pallas_call(pass_on, out_shape=tuple((jax.ShapeDtypeStruct(r.shape, r....  1.09 us

profile of v7, /device:TPU:1, one launch (start us, length us, event | category | flops | bytes accessed | tf_op | source)
XLA Modules:
  0.0 51.5 jit_solution(9641534372592694700)
XLA Ops:
  0.6 49.7 %shard_map.174 = (bf16[1024,128]{1,0:T(8,128)(2,1)S(1)}, f32[1024,128]{1,0:T(8,128)S(1)}, f32[8,128,128]{2,1,0:T(8,128)S(1)}, f32[2,128]{1,0:T(2,128)S(1)}) custom-call(bf16[1024,128]{1,0:T(8,128)(2,1)} %refs_0_.1, bf16[1024,128]{1,0:T(8,128)(2,1)} %refs_1_.1, s32[16,1024]{1,0:T(8,128)} %bitcast.4, s32[4,64]{1,0:T(4,128)} %refs_3_.1, s32[1,1024]{1,0:T(1,128)} %bitcast.5, ...), custom_call_target="tpu_custom_call" | custom-call | tf_op jit(solution)/shard_map/pallas_call | solution.py:602
  50.3 1.1 %shard_map.175 = (bf16[1024,128]{1,0:T(8,128)(2,1)}, f32[1024,128]{1,0:T(8,128)}, f32[8,128,128]{2,1,0:T(8,128)}, f32[2,128]{1,0:T(2,128)}) custom-call(bf16[1024,128]{1,0:T(8,128)(2,1)S(1)} %get-tuple-element.8.refs_0_, f32[1024,128]{1,0:T(8,128)S(1)} %get-tuple-element.9.refs_1_, f32[8,128,128]{2,1,0:T(8,128)S(1)} %get-tuple-element.10.refs_2_, ...), custom_call_target="tpu_custom_call" | custom-call | tf_op jit(solution)/shard_map/pallas_call | solution.py:619

commit v8 on v7

--- a/solution.py
+++ b/solution.py
@@ -297,11 +297,16 @@
         forward(u, 0)
     for k in (1, 3):
         node_forward(k, 0)
-    halo[0].wait()
-    halo[1].wait()
-    ghost_tables(0)
-    for u in (0, 1, 4, 5):
-        forward(u, 0)
+    for side in (1 - z_high, z_high):
+        here = pl.ds(pl.multiple_of(side * W, W), W)
+        pltpu.make_async_copy(ghost.at[here], ghost.at[here], halo_r.at[side]).wait()
+        own = ghost[here, :]
+        gtab[:, here] = nt(wsend_t, own).astype(BF16)
+        gtab_sh[:, here] = nt(wsend_t, jnp.concatenate([own[TILE:, :], own[:TILE, :]], axis=0)).astype(BF16)
+        forward(side, 0)
+        forward(side + 4, 0)
+    halo[0].wait_send()
+    halo[1].wait_send()
 
     for k in (0, 2):
         node_forward(k, 0)

time: 51.6 us -> 51.8 us (level)
  no operation moved by 1% of the time
where the time goes in v8:
time: 51.8 us; the launch traced here: 51.7 us
  Pallas kernels  50.9 us (98%)
  between operations  0.81 us (2%)
    pallas_call x1, Pallas kernels, step(): pl.pallas_call(functools.partial(kernel, sizes), out_shape=(jax.ShapeDtyp...  49.8 us
    pallas_call x1, Pallas kernels, step(): pl.pallas_call(pass_on, out_shape=tuple((jax.ShapeDtypeStruct(r.shape, r....  1.09 us

profile of v8, /device:TPU:1, one launch (start us, length us, event | category | flops | bytes accessed | tf_op | source)
XLA Modules:
  0.0 51.7 jit_solution(4669840558222622048)
XLA Ops:
  0.6 49.8 %shard_map.174 = (bf16[1024,128]{1,0:T(8,128)(2,1)S(1)}, f32[1024,128]{1,0:T(8,128)S(1)}, f32[8,128,128]{2,1,0:T(8,128)S(1)}, f32[2,128]{1,0:T(2,128)S(1)}) custom-call(bf16[1024,128]{1,0:T(8,128)(2,1)} %refs_0_.1, bf16[1024,128]{1,0:T(8,128)(2,1)} %refs_1_.1, s32[16,1024]{1,0:T(8,128)} %bitcast.4, s32[4,64]{1,0:T(4,128)} %refs_3_.1, s32[1,1024]{1,0:T(1,128)} %bitcast.5, ...), custom_call_target="tpu_custom_call" | custom-call | tf_op jit(solution)/shard_map/pallas_call | solution.py:607
  50.5 1.1 %shard_map.175 = (bf16[1024,128]{1,0:T(8,128)(2,1)}, f32[1024,128]{1,0:T(8,128)}, f32[8,128,128]{2,1,0:T(8,128)}, f32[2,128]{1,0:T(2,128)}) custom-call(bf16[1024,128]{1,0:T(8,128)(2,1)S(1)} %get-tuple-element.8.refs_0_, f32[1024,128]{1,0:T(8,128)S(1)} %get-tuple-element.9.refs_1_, f32[8,128,128]{2,1,0:T(8,128)S(1)} %get-tuple-element.10.refs_2_, ...), custom_call_target="tpu_custom_call" | custom-call | tf_op jit(solution)/shard_map/pallas_call | solution.py:624
